TPU v7x, 128 devices: a whole 4x4x4 slice. The times are simulated.
128 devices in a mesh: group: 4 (over y_hi, core), fsdp: 32 (over y_lo, x, z).
Axes of the slice: x: 4, y: 4 (y_hi: 2, y_lo: 2; y = y_hi * 2 + y_lo), z: 4, core: 2. Of those that a mesh axis runs over, the one named last changes fastest.
Arguments:
- hidden: bfloat16 [4, 64, 256, 5120], P('group', 'fsdp'), may hold values from -600 to 600
- norm_gain: float32 [5120], replicated, may hold values from 0.1 to 1.9
- queries: bfloat16 [4, 64, 256, 2560], P('group', 'fsdp'), may hold values from -800 to 800
- out_grad: bfloat16 [4, 64, 256, 2560], P('group', 'fsdp'), may hold values from -6 to 6
- kv_inner: bfloat16 [4, 5120, 1024], P('group', 'fsdp'), may hold values from -6 to 6
- kv_outer: float32 [5120, 1024], P('fsdp'), may hold values from -6 to 6
- momentum: float32 [5120, 1024], P('fsdp'), may hold values from -2 to 2
Outputs:
- blended: bfloat16 [4, 5120, 1024], P('group', 'fsdp')
- outer_new: float32 [5120, 1024], P('fsdp')
- momentum_new: float32 [5120, 1024], P('fsdp')
All inputs are finite; a program needn't handle non-finite values. Where the computation divides by a largest or mean magnitude, that divisor is 1e-20 or more.
Results may differ from a plain program's by a relative error of at most 0.025.
The roundings to bfloat16 on the way count: a program that leaves them out, or rounds other values in their place, can miss the bound.
Values may be sent and summed in bfloat16 or wider, within the bound.
A program may use at most 128 MiB of HBM per device.

v0:
```python
import jax
import jax.numpy as jnp
from jax import lax
from jax.sharding import Mesh
from jax.sharding import PartitionSpec as P

D = 5120
HD = 128
QBLOCK = 128
FSDP = ("fsdp_0", "fsdp_1", "fsdp_2")


inner_rate = 0.25
outer_rate = 0.7
momentum_decay = 0.9
blend_share = 0.5
norm_eps = 1e-06
scale_eps = 1e-06


def reduced_to_own(tiles, axes, turns):
    shape = [lax.axis_size(a) for a in axes]
    tiles = tiles.reshape(*shape, *tiles.shape[1:])
    tiles = tiles.transpose(*turns, *range(len(axes), tiles.ndim))
    tiles = tiles.reshape(-1, *tiles.shape[len(axes) :])
    for k in turns:
        tiles = lax.psum_scatter(tiles, axes[k], scatter_dimension=0, tiled=True)
    return tiles[0]


def in_blocks(value, dim, length):
    shape = value.shape
    tiles = value.reshape(*shape[:dim], length, shape[dim] // length, *shape[dim + 1 :])
    return jnp.moveaxis(tiles, dim, 0)


def scatter_axes(value, axes, turns, dim):
    length = lax.axis_size(axes)
    return reduced_to_own(in_blocks(value, dim, length), axes, turns)


def laid_out(tiles, dim):
    tiles = jnp.moveaxis(tiles, 0, dim)
    shape = tiles.shape
    return tiles.reshape(*shape[:dim], shape[dim] * shape[dim + 1], *shape[dim + 2 :])


def sent_to_all(value, axis):
    copies = jnp.broadcast_to(value, (lax.axis_size(axis), *value.shape))
    return lax.all_to_all(copies, axis, split_axis=0, concat_axis=0, tiled=True)


def gather_directly(value, axis, dim):
    return laid_out(sent_to_all(value, axis), dim)


def side_by_side(arrays, axis, dim, along):
    both = jnp.concatenate(arrays, axis=along)
    out, at, finished = (gather_directly(both, axis, dim), 0, [])
    for a in arrays:
        finished.append(lax.slice_in_dim(out, at, at + a.shape[along], axis=along))
        at += a.shape[along]
    return tuple(finished)


def normed_rows(hidden_rows, norm_gain):
    looked = hidden_rows.reshape(-1, hidden_rows.shape[-1]).astype(jnp.float32)
    mean_sq = jnp.mean(looked * looked, axis=-1, keepdims=True)
    return (looked * lax.rsqrt(mean_sq + norm_eps) * norm_gain).astype(jnp.bfloat16)


def attend(queries, kv_rows):
    seq_count, length, query_width = queries.shape
    kv_width = kv_rows.shape[-1] // 2
    kv_heads = kv_width // HD
    repeat = query_width // (kv_heads * HD)
    query_h = queries.reshape(seq_count, length, kv_heads, repeat, HD)
    key_h = kv_rows[..., :kv_width].reshape(seq_count, length, kv_heads, HD)
    value_h = kv_rows[..., kv_width:].reshape(seq_count, length, kv_heads, HD)
    scores = jnp.einsum(
        "slgrd,smgd->sgrlm", query_h, key_h, preferred_element_type=jnp.float32
    ) * HD ** (-0.5)
    places = jnp.arange(length)
    causal = places[None, :] <= places[:, None]
    scores = jnp.where(causal, scores, -1e30)
    highest = lax.stop_gradient(jnp.max(scores, axis=-1, keepdims=True))
    exp_scores = jnp.exp(scores - highest)
    prob_rows = (exp_scores / jnp.sum(exp_scores, axis=-1, keepdims=True)).astype(jnp.bfloat16)
    mixed_out = jnp.einsum(
        "sgrlm,smgd->slgrd", prob_rows, value_h, preferred_element_type=jnp.float32
    )
    return mixed_out.reshape(seq_count, length, query_width)


def kv_grads(queries, kv_rows, out_grad):

    def loss_part(kv_value):
        return attend(queries, kv_value)

    _, pullback = jax.vjp(loss_part, kv_rows)
    return pullback(out_grad.astype(jnp.float32))[0]


def quantize(delta):
    row_count = delta.shape[0]
    shaped = delta.reshape(row_count, -1, QBLOCK)
    scales = (jnp.max(jnp.abs(shaped), axis=-1) + scale_eps).astype(jnp.bfloat16)
    coded = (shaped / scales.astype(jnp.float32)[..., None]).astype(jnp.bfloat16)
    return (coded.reshape(row_count, -1), scales)


def dequantize(coded, scales):
    row_count = coded.shape[0]
    shaped = coded.reshape(row_count, scales.shape[1], -1).astype(jnp.float32)
    return (shaped * scales.astype(jnp.float32)[..., None]).reshape(row_count, -1)


def nesterov(outer_rows, moment_rows, average):
    moment_next = momentum_decay * moment_rows + average
    outer_next = outer_rows - outer_rate * (momentum_decay * moment_next + average)
    return (outer_next, moment_next)


def grad_term(rows_in, kv_part, inv_root):
    product = lax.dot_general(
        rows_in, kv_part, (((0,), (0,)), ((), ())), preferred_element_type=jnp.float32
    )
    return product * inv_root


def local(hidden, norm_gain, queries, out_grad, kv_inner, kv_outer, momentum):
    inv_root = D ** (-0.5)
    groups = lax.axis_size("group")
    rows_in = normed_rows(hidden[0], norm_gain)
    local_weights = kv_inner[0]
    kv_cols = local_weights.shape[1]
    projected = jnp.dot(
        rows_in,
        lax.all_gather(local_weights, FSDP, axis=0, tiled=True),
        preferred_element_type=jnp.float32,
    )
    kv_rows = (projected * inv_root).astype(jnp.bfloat16)
    seq_local = queries.shape[1]
    kv_rows = kv_rows.reshape(seq_local, queries.shape[2], kv_cols)
    kv_grad = kv_grads(queries[0], kv_rows, out_grad[0]).reshape(-1, kv_cols)
    gradient = scatter_axes(
        grad_term(rows_in, kv_grad, inv_root).astype(jnp.bfloat16), FSDP, (1, 2, 0), 0
    ).astype(jnp.float32)
    fresh = local_weights.astype(jnp.float32) - inner_rate * gradient
    coded, scales = quantize(kv_outer - fresh)
    all_coded, all_scales = side_by_side((coded[None], scales[None]), "group", 0, 2)
    totals = jnp.zeros(kv_outer.shape, jnp.float32)
    for member in range(groups):
        totals = totals + dequantize(all_coded[member], all_scales[member])
    average = totals / groups
    outer_new, momentum_new = nesterov(kv_outer, momentum, average)
    blended = (blend_share * fresh + (1.0 - blend_share) * outer_new).astype(jnp.bfloat16)
    return (blended[None], outer_new, momentum_new)


def solution(mesh):
    split = Mesh(
        mesh.devices.reshape(mesh.shape["group"], 2, 4, 4), ("group", "fsdp_0", "fsdp_1", "fsdp_2")
    )
    return jax.shard_map(
        local,
        mesh=split,
        in_specs=(
            P("group", FSDP, None, None),
            P(),
            P("group", FSDP, None, None),
            P("group", FSDP, None, None),
            P("group", FSDP, None),
            P(FSDP, None),
            P(FSDP, None),
        ),
        out_specs=(P("group", FSDP, None), P(FSDP, None), P(FSDP, None)),
        check_vma=False,
    )
```

profile of v0, /device:TPU:1, one launch (start us, length us, event | category | flops | bytes accessed | tf_op | source)
XLA Modules:
  0.0 438.3 jit_solution(1444082924454588420)
XLA Ops:
  7.2 0.0 copy-start.9
  7.2 0.0 all-gather.3.cloned.1.call-start
  7.2 0.7 all-gather.3.cloned.1.call-update
  7.9 0.0 reduce-scatter.4.cloned.1.call-start
  8.0 3.6 multiply_reduce_fusion
  11.6 0.0 slice-start
  11.6 4.5 %copy.27 = bf16[1,2,256,2560]{2,3,1,0:T(8,128)(2,1)} copy(bf16[1,2,256,2560]{3,2,1,0:T(8,128)(2,1)} %param.9) | data formatting | bytes 5242880 | tf_op args[2]
  16.1 4.4 %copy.30 = bf16[1,2,256,2560]{2,3,1,0:T(8,128)(2,1)} copy(bf16[1,2,256,2560]{3,2,1,0:T(8,128)(2,1)} %param.10) | data formatting | bytes 5242880 | tf_op args[3]
  20.5 0.0 slice-start.1
  20.6 0.0 copy-done.9
  20.6 7.0 %fusion.11 = bf16[512,5120]{1,0:T(8,128)(2,1)} fusion(f32[5120]{0:T(1024)S(1)} %copy-done.9, f32[512]{0:T(512)S(1)} %bitcast.245, bf16[1,2,256,5120]{3,2,1,0:T(8,128)(2,1)} %param.7), kind=kLoop, calls=%fused_computation.16 | loop fusion | flops 10485760 | bytes 10508288 | tf_op jit(solution)/shard_map/convert_element_type | solution.py:69
  27.5 0.0 slice-done
  27.5 0.0 slice-done.1
  27.5 4.3 multiply_convert_fusion.1
  31.9 131.2 %all-gather.3.cloned.1.call-done = bf16[1,5120,1024]{2,1,0:T(8,128)(2,1)} async-done(((bf16[1,160,1024]{2,1,0:T(8,128)(2,1)}), bf16[1,5120,1024]{2,1,0:T(8,128)(2,1)}) %all-gather.3.cloned.1.call-update) | async-done | bytes 10485776 | tf_op jit(solution)/shard_map/all_gather | solution.py:139
  163.1 10.0 %multiply_convert_fusion.2 = bf16[512,1024]{1,0:T(8,128)(2,1)S(1)} fusion(bf16[512,5120]{1,0:T(8,128)(2,1)} %fusion.11, bf16[1,5120,1024]{2,1,0:T(8,128)(2,1)} %all-gather.3.cloned.1.call-done), kind=kOutput, calls=%fused_computation.34 | convolution fusion | flops 5369757696 | bytes 16777216 | tf_op jit(solution)/shard_map/dot_general | solution.py:137
  173.1 0.9 fusion.56
  174.0 2.0 copy.47
  176.0 0.0 copy-done.1
  176.0 2.9 fusion.14
  178.9 0.0 copy-start
  178.9 4.0 copy-done
  182.9 2.6 fusion.16
  185.5 0.0 slice-start.2
  185.5 1.0 copy.48
  186.5 7.7 %fusion.34 = bf16[2,4,256,128]{2,3,1,0:T(8,128)(2,1)S(1)} fusion(bf16[2,4,128,5,256]{4,2,3,1,0:T(8,128)(2,1)} %bitcast.233, f32[2,4,256,256,5]{3,2,4,1,0:T(8,128)} %copy-done, f32[2,4,5,256]{3,2,1,0:T(8,128)S(1)} %fusion.16, f32[2,4,5,256]{3,2,1,0:T(8,128)S(1)} %get-tuple-element.16, pred[256,256]{0,1:T(8,128)(4,1)S(1)} %iota_compare_fusion.1), kind=kOutput, calls=%fused_computation.38 | convolution fusion | flops 684457984 | bytes 13778944 | tf_op jit(solution)/shard_map/transpose(jvp(sgrlm,smgd->slgrd))/dot_general | solution.py:89
  194.2 0.0 slice-done.2
  194.2 0.0 slice-done.3
  194.2 0.0 slice-done.4
  194.2 0.3 copy-done.6
  194.5 0.0 copy-done.8
  194.6 5.3 %fusion.7 = (f32[2,4,5,256]{3,2,1,0:T(8,128)S(1)}, bf16[2,4,256,5,256]{4,2,3,1,0:T(8,128)(2,1)}) fusion(f32[2,4,256,256,5]{3,2,4,1,0:T(8,128)S(1)} %bitcast.222, f32[2,4,5,256]{3,2,1,0:T(8,128)S(1)} %multiply_divide_fusion, f32[2,4,5,256]{3,2,1,0:T(8,128)S(1)} %get-tuple-element.16, pred[256,256]{0,1:T(8,128)(4,1)S(1)} %iota_compare_fusion.1, ...), kind=kOutput, calls=%fused_computation.10 | convolution fusion | flops 692049920 | bytes 19062784 | tf_op jit(solution)/shard_map/transpose(jvp(sgrlm,smgd->slgrd))/dot_general | solution.py:89
  199.8 0.0 copy-done.2
  199.8 6.5 %fusion.31 = bf16[2,4,256,128]{2,3,1,0:T(8,128)(2,1)S(1)} fusion(bf16[2,256,4,5,128]{1,4,3,2,0:T(8,128)(2,1)S(1)} %bitcast.225, bf16[2,4,256,5,256]{4,2,3,1,0:T(8,128)(2,1)} %get-tuple-element.19, f32[2,4,256,256,5]{3,2,4,1,0:T(8,128)S(1)} %bitcast.222, f32[2,4,256,5]{2,3,1,0:T(8,128)S(1)} %bitcast.243, f32[2,4,256,5]{2,3,1,0:T(8,128)S(1)} %negate_bitcast_fusion, ...), kind=kOutput, calls=%fused_computation.37 | convolution fusion | flops 694943744 | bytes 19062784 | tf_op jit(solution)/shard_map/transpose(jvp(slgrd,smgd->sgrlm))/dot_general | solution.py:80
  206.4 0.2 copy.35
  206.6 0.2 copy.32
  206.8 0.1 pad_add_fusion
  206.9 10.9 %multiply_convert_fusion = bf16[5120,1024]{1,0:T(8,128)(2,1)} fusion(bf16[512,5120]{1,0:T(8,128)(2,1)} %bitcast.228, bf16[512,1024]{1,0:T(8,128)(2,1)S(1)} %bitcast.239), kind=kOutput, calls=%fused_computation | convolution fusion | flops 5379194880 | bytes 16777216 | tf_op jit(solution)/shard_map/dot_general | solution.py:125
  217.8 9.8 %copy.36 = bf16[4,4,2,160,1024]{4,3,2,1,0:T(8,128)(2,1)} copy(bf16[4,4,2,160,1024]{4,3,1,0,2:T(8,128)(2,1)} %bitcast.223) | data formatting | bytes 20971520 | tf_op jit(solution)/shard_map/transpose | solution.py:24
  227.7 0.0 reduce-scatter.4.cloned.1.call-update
  227.7 0.0 copy-start.7
  227.7 0.0 reduce-scatter.6.cloned.1.call-start
  227.8 116.3 %reduce-scatter.4.cloned.1.call-done = bf16[8,160,1024]{2,1,0:T(8,128)(2,1)} async-done(((bf16[32,160,1024]{2,1,0:T(8,128)(2,1)}), bf16[8,160,1024]{2,1,0:T(8,128)(2,1)}) %reduce-scatter.4.cloned.1.call-update) | async-done | bytes 2621456 | tf_op jit(solution)/shard_map/reduce_scatter | solution.py:27
  344.1 0.0 reduce-scatter.6.cloned.1.call-update
  344.1 0.0 reduce-scatter.8.cloned.1.call-start
  344.2 36.3 %reduce-scatter.6.cloned.1.call-done = bf16[2,160,1024]{2,1,0:T(8,128)(2,1)} async-done(((bf16[8,160,1024]{2,1,0:T(8,128)(2,1)}), bf16[2,160,1024]{2,1,0:T(8,128)(2,1)}) %reduce-scatter.6.cloned.1.call-update) | async-done | bytes 655376 | tf_op jit(solution)/shard_map/reduce_scatter | solution.py:27
  380.5 0.0 reduce-scatter.8.cloned.1.call-update
  380.6 20.3 %reduce-scatter.8.cloned.1.call-done = bf16[1,160,1024]{2,1,0:T(8,128)(2,1)} async-done(((bf16[2,160,1024]{2,1,0:T(8,128)(2,1)}), bf16[1,160,1024]{2,1,0:T(8,128)(2,1)}) %reduce-scatter.8.cloned.1.call-update) | async-done | bytes 327696 | tf_op jit(solution)/shard_map/reduce_scatter | solution.py:27
  400.8 0.0 copy-done.3
  400.8 0.0 copy-done.4
  400.9 1.2 abs_bitcast_fusion
  402.0 0.1 copy.50
  402.2 0.2 reduce_max.19
  402.4 0.2 div.57
  402.7 1.3 fusion.43
  404.0 0.1 broadcast_in_dim.49
  404.1 24.6 %all_to_all.5 = bf16[4,1,160,1032]{3,2,1,0:T(8,128)(2,1)S(1)} all-to-all(bf16[4,1,160,1032]{3,2,1,0:T(8,128)(2,1)S(1)} %broadcast_in_dim.49), channel_id=1, replica_groups=mesh['group'=4,'fsdp_0'=2,'fsdp_1'=4,'fsdp_2'=4] {'group'}, dimensions={0} | all-to-all | bytes 2641920 | tf_op jit(solution)/shard_map/all_to_all | solution.py:50
  428.7 0.2 mul.176
  428.9 0.2 mul.179
  429.2 0.2 mul.182
  429.4 0.2 mul.185
  429.6 0.0 copy-done.7
  429.6 0.0 copy-done.5
  429.6 2.1 fusion.42
  (20 shorter events, 0.2 us)
Async XLA Ops:
  7.2 13.4 %copy-start.9 = (f32[5120]{0:T(1024)S(1)}, f32[5120]{0:T(1024)}, u32[]{:S(2)}) copy-start(f32[5120]{0:T(1024)} %param.8) | copy-start | bytes 61444
  7.2 155.9 %all-gather.3.cloned.1.call-start = ((), (), s32[]{:S(2)}) async-start(), calls=%async_computation.7 | async-start | bytes 10813440 | tf_op jit(solution)/shard_map/all_gather | solution.py:139
  7.9 336.2 %reduce-scatter.4.cloned.1.call-start = ((), (), s32[]{:S(2)}) async-start(), calls=%async_computation.4 | async-start | bytes 13107200 | tf_op jit(solution)/shard_map/reduce_scatter | solution.py:27
  11.6 16.0 %slice-start = ((s8[5242880]{0:T(1024)(128)(4,1)}), s8[1048576]{0:T(1024)(128)(4,1)S(1)}, s32[]{:S(2)}) async-start(s8[5242880]{0:T(1024)(128)(4,1)} %bitcast.218), calls=%async_computation.8 | async-start | bytes 2097152
  20.5 7.0 %slice-start.1 = ((s8[5242880]{0:T(1024)(128)(4,1)}), s8[4194304]{0:T(1024)(128)(4,1)S(1)}, s32[]{:S(2)}) async-start(s8[5242880]{0:T(1024)(128)(4,1)} %bitcast.218), calls=%async_computation.9 | async-start | bytes 8388608
  31.9 144.2 %copy-start.1 = (bf16[1,2,256,2560]{2,3,1,0:T(8,128)(2,1)S(1)}, bf16[1,2,256,2560]{2,3,1,0:T(8,128)(2,1)}, u32[]{:S(2)}) copy-start(bf16[1,2,256,2560]{2,3,1,0:T(8,128)(2,1)} %copy.27) | copy-start | bytes 7864324
  178.9 4.0 copy-start
  185.5 8.7 %slice-start.2 = ((s8[10485760]{0:T(1024)(128)(4,1)}), s8[2097152]{0:T(1024)(128)(4,1)S(1)}, s32[]{:S(2)}) async-start(s8[10485760]{0:T(1024)(128)(4,1)} %bitcast.221), calls=%async_computation.10 | async-start | bytes 4194304
  186.5 7.7 %slice-start.3 = ((s8[10485760]{0:T(1024)(128)(4,1)}), s8[4194304]{0:T(1024)(128)(4,1)S(1)}, s32[]{:S(2)}) async-start(s8[10485760]{0:T(1024)(128)(4,1)} %bitcast.221), calls=%async_computation.11 | async-start | bytes 8388608
  186.5 7.7 %slice-start.4 = ((s8[10485760]{0:T(1024)(128)(4,1)}), s8[4194304]{0:T(1024)(128)(4,1)S(1)}, s32[]{:S(2)}) async-start(s8[10485760]{0:T(1024)(128)(4,1)} %bitcast.221), calls=%async_computation.12 | async-start | bytes 8388608
  186.5 8.0 %copy-start.6 = (bf16[1,2,256,2560]{2,3,1,0:T(8,128)(2,1)S(1)}, bf16[1,2,256,2560]{2,3,1,0:T(8,128)(2,1)}, u32[]{:S(2)}) copy-start(bf16[1,2,256,2560]{2,3,1,0:T(8,128)(2,1)} %copy.30) | copy-start | bytes 7864324
  186.5 8.1 %copy-start.8 = (bf16[2,256,512]{1,2,0:T(8,128)(2,1)S(1)}, bf16[2,256,512]{1,2,0:T(8,128)(2,1)}, u32[]{:S(2)}) copy-start(bf16[2,256,512]{1,2,0:T(8,128)(2,1)} %copy.48) | copy-start | bytes 1572868
  194.5 5.3 %copy-start.2 = (bf16[1,2,256,2560]{2,3,1,0:T(8,128)(2,1)S(1)}, bf16[1,2,256,2560]{2,3,1,0:T(8,128)(2,1)}, u32[]{:S(2)}) copy-start(bf16[1,2,256,2560]{2,3,1,0:T(8,128)(2,1)} %copy.27) | copy-start | bytes 7864324
  227.7 173.2 %copy-start.3 = (f32[160,1024]{1,0:T(8,128)S(1)}, f32[160,1024]{1,0:T(8,128)}, u32[]{:S(2)}) copy-start(f32[160,1024]{1,0:T(8,128)} %param.12) | copy-start | bytes 1966084
  227.7 173.2 %copy-start.4 = (bf16[1,160,1024]{2,1,0:T(8,128)(2,1)S(1)}, bf16[1,160,1024]{2,1,0:T(8,128)(2,1)}, u32[]{:S(2)}) copy-start(bf16[1,160,1024]{2,1,0:T(8,128)(2,1)} %param.11) | copy-start | bytes 983044
  227.7 201.9 %copy-start.7 = (f32[160,1024]{1,0:T(8,128)S(1)}, f32[160,1024]{1,0:T(8,128)}, u32[]{:S(2)}) copy-start(f32[160,1024]{1,0:T(8,128)} %param.13) | copy-start | bytes 1966084
  227.7 152.8 %reduce-scatter.6.cloned.1.call-start = ((), (), s32[]{:S(2)}) async-start(), calls=%async_computation.5 | async-start | bytes 3276800 | tf_op jit(solution)/shard_map/reduce_scatter | solution.py:27
  344.1 56.7 %reduce-scatter.8.cloned.1.call-start = ((), (), s32[]{:S(2)}) async-start(), calls=%async_computation.6 | async-start | bytes 983040 | tf_op jit(solution)/shard_map/reduce_scatter | solution.py:27
  400.9 28.8 %copy-start.5 = (bf16[1,160,1024]{2,1,0:T(8,128)(2,1)S(1)}, bf16[1,160,1024]{2,1,0:T(8,128)(2,1)}, u32[]{:S(2)}) copy-start(bf16[1,160,1024]{2,1,0:T(8,128)(2,1)} %reduce-scatter.8.cloned.1.call-done) | copy-start | bytes 983044
Sparse Core Ops, SparseCore 0:
  9.6 153.4 all-gather.2
  227.8 116.2 reduce-scatter.3
  346.5 33.9 reduce-scatter.5
  382.7 18.0 reduce-scatter.7
where the time goes:
time: 439 us; the launch traced here: 438 us
  waiting for transfers between devices  305 us (69%)
  matrix products  43.3 us (10%)
  local copies, waits for them, and re-layouts  28.8 us (7%)
  blocking collectives  24.6 us (6%)
  other arithmetic  22.4 us (5%)
  between operations  14 us (3%)
    reduce_scatter x3, waiting for transfers between devices, reduced_to_own(): tiles = lax.psum_scatter(tiles, axes[k], scatter_dimension=0, tiled=True)  173 us
    all_gather x1, waiting for transfers between devices, local(): lax.all_gather(local_weights, FSDP, axis=0, tiled=True)  131 us
    all_to_all x1, blocking collectives, sent_to_all(): return lax.all_to_all(copies, axis, split_axis=0, concat_axis=0, tiled=True)  24.6 us
    unnamed x36, local copies, waits for them, and re-layouts  16.4 us
    dot_general x2, matrix products, attend(): jnp.einsum('sgrlm,smgd->slgrd', prob_rows, value_h, preferred_element_typ...  13 us
    convert_element_type x2, other arithmetic, normed_rows(): (looked * lax.rsqrt(mean_sq + norm_eps) * norm_gain).astype(jnp.bfloat16)  11.3 us
    dot_general x1, matrix products, grad_term(): lax.dot_general(rows_in, kv_part, (((0,), (0,)), ((), ())), preferred_ele...  10.9 us
    dot_general x1, matrix products, local(): jnp.dot(rows_in, lax.all_gather(local_weights, FSDP, axis=0, tiled=True),...  10 us
  transfers between devices with their start and end apart: 4, of which 4 were waited for; matrix products, arithmetic and copies ran while one was open for 5% of the time, Pallas kernels for 0%

commit v1 on v0

--- a/solution.py
+++ b/solution.py
@@ -1,13 +1,23 @@
+import functools
 import jax
 import jax.numpy as jnp
 from jax import lax
+from jax.experimental import pallas as pl
+from jax.experimental.pallas import tpu as pltpu
 from jax.sharding import Mesh
 from jax.sharding import PartitionSpec as P
 
 D = 5120
 HD = 128
+KVC = 1024
+TOK = 512
+ROWS = 160
 QBLOCK = 128
-FSDP = ("fsdp_0", "fsdp_1", "fsdp_2")
+GROUP = ("hi", "core")
+FSDP = ("lo", "x", "z")
+MESH = pl.DeviceIdType.MESH
+BF = jnp.bfloat16
+F32 = jnp.float32
 
 
 inner_rate = 0.25
@@ -16,6 +26,252 @@
 blend_share = 0.5
 norm_eps = 1e-06
 scale_eps = 1e-06
+
+
+def piece_cols(p):
+    return (p // 2) * 128 + (p % 2) * 512
+
+
+class Place:
+    def __init__(self):
+        self.y = lax.axis_index("lo")
+        self.x = lax.axis_index("x")
+        self.z = lax.axis_index("z")
+        self.yo = 1 - self.y
+
+    def names(self, p):
+        return ("x", "z") if p % 2 == 0 else ("z", "x")
+
+    def at(self, p, first, off):
+        v = getattr(self, self.names(p)[0 if first else 1])
+        return lax.rem(v + (off + 4), 4)
+
+    def dev(self, p, first, off):
+        return {self.names(p)[0 if first else 1]: self.at(p, first, off)}
+
+    def row(self, ref, p, y, c_off):
+        c = self.at(p, False, c_off)
+        if p % 2 == 0:
+            return ref.at[p, y, :, c]
+        return ref.at[p, y, c]
+
+    def block(self, ref, p, y, a_off, c_off):
+        a, c = self.at(p, True, a_off), self.at(p, False, c_off)
+        if p % 2 == 0:
+            return ref.at[p, y, a, c]
+        return ref.at[p, y, c, a]
+
+
+def remote(src, dst, send, recv, dev):
+    return pltpu.make_async_remote_copy(
+        src_ref=src, dst_ref=dst, send_sem=send, recv_sem=recv, device_id=dev, device_id_type=MESH
+    )
+
+
+def meet(devs):
+    barrier = pltpu.get_barrier_semaphore()
+    for dev in devs:
+        pl.semaphore_signal(barrier, inc=1, device_id=dev, device_id_type=MESH)
+    pl.semaphore_wait(barrier, len(devs))
+
+
+class Gather:
+    def __init__(self, place, w8, send, recv):
+        self.place, self.w8, self.send, self.recv = place, w8, send, recv
+
+    def copy(self, p, k):
+        pc, w = self.place, self.w8
+        plus = (p // 2) % 2 == 0
+        src, dev = {
+            0: lambda: (pc.block(w, p, pc.y, 0, 0), pc.dev(p, True, 1)),
+            1: lambda: (pc.block(w, p, pc.y, 0, 0), pc.dev(p, True, -1)),
+            2: lambda: (
+                pc.block(w, p, pc.y, -1 if plus else 1, 0),
+                pc.dev(p, True, 1 if plus else -1),
+            ),
+            3: lambda: (pc.row(w, p, pc.y, 0), {"lo": pc.yo}),
+            4: lambda: (pc.row(w, p, pc.y, 0), pc.dev(p, False, 1)),
+            5: lambda: (pc.row(w, p, pc.yo, 0), pc.dev(p, False, 1)),
+            6: lambda: (pc.row(w, p, pc.y, 0), pc.dev(p, False, -1)),
+            7: lambda: (pc.row(w, p, pc.yo, 0), pc.dev(p, False, -1)),
+            8: lambda: (pc.row(w, p, pc.y, -1), pc.dev(p, False, 1)),
+            9: lambda: (pc.row(w, p, pc.yo, 1), pc.dev(p, False, -1)),
+        }[k]()
+        return remote(src, src, self.send.at[p, k], self.recv.at[p, k], dev)
+
+    def start(self, p, k):
+        self.copy(p, k).start()
+
+    def landed(self, p, k):
+        self.copy(p, k).wait_recv()
+
+    def stage(self, p, s):
+        start, landed = functools.partial(self.start, p), functools.partial(self.landed, p)
+        if s == 0:
+            start(0)
+            start(1)
+        elif s == 1:
+            landed(0)
+            landed(1)
+            start(2)
+        elif s == 2:
+            landed(2)
+            start(3)
+            start(4)
+            start(6)
+        elif s == 3:
+            landed(3)
+            start(5)
+            start(7)
+            landed(4)
+            start(8)
+        elif s == 4:
+            landed(7)
+            start(9)
+        elif s == 5:
+            for k in (5, 6, 8, 9):
+                landed(k)
+
+    def drain(self):
+        for p in range(8):
+            for k in range(10):
+                self.copy(p, k).wait_send()
+
+
+def norm_rows(rows, gain, start, count):
+    def step(i, carry):
+        at = pl.ds(pl.multiple_of(start + i * 16, 16), 16)
+        looked = rows[at, :].astype(F32)
+        mean_sq = jnp.mean(looked * looked, axis=-1, keepdims=True)
+        looked = rows[at, :].astype(F32)
+        rows[at, :] = (looked * lax.rsqrt(mean_sq + norm_eps) * gain[...]).astype(BF)
+        return carry
+
+    lax.fori_loop(0, count // 16, step, 0)
+
+
+def turn_rows(rows, rows_t, start, count):
+    def step(j, carry):
+        at = pl.multiple_of((start + j) * 128, 128)
+        rows_t[pl.ds(at, 128), :] = rows[:, pl.ds(at, 128)].T
+        return carry
+
+    lax.fori_loop(0, count, step, 0)
+
+
+def project(rows, w8, acc, kv, h):
+    inv_root = D ** (-0.5)
+
+    def step(i, carry):
+        at = pl.multiple_of(i * 1280, 1280)
+        y, x = i // 2, 2 * lax.rem(i, 2)
+        pair = [w8[2 * h + e, y, pl.ds(x, 2)].reshape(1280, 128) for e in range(2)]
+        acc[...] += jnp.dot(
+            rows[:, pl.ds(at, 1280)],
+            jnp.concatenate(pair, axis=1),
+            preferred_element_type=F32,
+        )
+        return carry
+
+    acc[...] = jnp.zeros_like(acc)
+    lax.fori_loop(0, 4, step, 0)
+    out = (acc[...] * inv_root).astype(BF)
+    kv[:, h * 128 : h * 128 + 128] = out[:, :128]
+    kv[:, 512 + h * 128 : 640 + h * 128] = out[:, 128:]
+
+
+def interleave(comm, work):
+    n = len(comm)
+    done = 0
+    for i, f in enumerate(comm):
+        f()
+        upto = (i + 1) * len(work) // n
+        for g in work[done:upto]:
+            g()
+        done = upto
+
+
+def project_kernel(
+    hidden, gain, w, kv, rows_t, rows, w8, acc, send, recv, load_sem, own_sem
+):
+    pc = Place()
+    ga = Gather(pc, w8, send, recv)
+    loads = []
+    for i in range(8):
+        at = slice(i * 64, i * 64 + 64)
+        loads.append(pltpu.make_async_copy(hidden.at[at], rows.at[at], load_sem.at[i]))
+    owns = []
+    for p in range(8):
+        c = piece_cols(p)
+        owns.append(
+            pltpu.make_async_copy(
+                w.at[:, c : c + 128], pc.block(w8, p, pc.y, 0, 0), own_sem.at[p]
+            )
+        )
+    for cp in owns:
+        cp.start()
+    for cp in loads:
+        cp.start()
+    meet(
+        [{"lo": pc.yo}]
+        + [pc.dev(p, True, o) for p in range(2) for o in (1, -1)]
+    )
+    for p in range(8):
+        owns[p].wait()
+        ga.stage(p, 0)
+
+    def norm(i):
+        loads[i].wait()
+        norm_rows(rows, gain, i * 64, 64)
+
+    def stage(s, h):
+        return [functools.partial(ga.stage, 2 * h + e, s) for e in range(2)]
+
+    first = (
+        stage(1, 0) + stage(2, 0) + stage(1, 1) + stage(3, 0) + stage(2, 1) + stage(4, 0)
+    )
+    interleave(first, [functools.partial(norm, i) for i in range(8)])
+    turns = [functools.partial(turn_rows, rows, rows_t, i * 5, 5) for i in range(8)]
+    interleave(stage(3, 1) + stage(1, 2) + stage(2, 2) + stage(4, 1) + stage(5, 0), turns[:4])
+    project(rows, w8, acc, kv, 0)
+    interleave(stage(3, 2) + stage(1, 3) + stage(2, 3) + stage(4, 2) + stage(5, 1), turns[4:])
+    project(rows, w8, acc, kv, 1)
+    interleave(stage(3, 3) + stage(4, 3) + stage(5, 2), [])
+    project(rows, w8, acc, kv, 2)
+    interleave(stage(5, 3), [])
+    project(rows, w8, acc, kv, 3)
+    ga.drain()
+
+
+def gathered_projection(hidden, gain, w):
+    return pl.pallas_call(
+        project_kernel,
+        out_shape=(
+            jax.ShapeDtypeStruct((TOK, KVC), BF),
+            jax.ShapeDtypeStruct((D, TOK), BF),
+        ),
+        in_specs=[
+            pl.BlockSpec(memory_space=pl.ANY),
+            pl.BlockSpec(memory_space=pltpu.VMEM),
+            pl.BlockSpec(memory_space=pl.ANY),
+        ],
+        out_specs=(
+            pl.BlockSpec(memory_space=pltpu.VMEM),
+            pl.BlockSpec(memory_space=pltpu.VMEM),
+        ),
+        scratch_shapes=[
+            pltpu.VMEM((TOK, D), BF),
+            pltpu.VMEM((8, 2, 4, 4, ROWS, 128), BF),
+            pltpu.VMEM((TOK, 256), F32),
+            pltpu.SemaphoreType.DMA((8, 10)),
+            pltpu.SemaphoreType.DMA((8, 10)),
+            pltpu.SemaphoreType.DMA((8,)),
+            pltpu.SemaphoreType.DMA((8,)),
+        ],
+        compiler_params=pltpu.CompilerParams(
+            collective_id=0, has_side_effects=True, vmem_limit_bytes=48 * 1024 * 1024
+        ),
+    )(hidden, gain, w)
 
 
 def reduced_to_own(tiles, axes, turns):
@@ -61,12 +317,6 @@
         finished.append(lax.slice_in_dim(out, at, at + a.shape[along], axis=along))
         at += a.shape[along]
     return tuple(finished)
-
-
-def normed_rows(hidden_rows, norm_gain):
-    looked = hidden_rows.reshape(-1, hidden_rows.shape[-1]).astype(jnp.float32)
-    mean_sq = jnp.mean(looked * looked, axis=-1, keepdims=True)
-    return (looked * lax.rsqrt(mean_sq + norm_eps) * norm_gain).astype(jnp.bfloat16)
 
 
 def attend(queries, kv_rows):
@@ -121,34 +371,22 @@
     return (outer_next, moment_next)
 
 
-def grad_term(rows_in, kv_part, inv_root):
-    product = lax.dot_general(
-        rows_in, kv_part, (((0,), (0,)), ((), ())), preferred_element_type=jnp.float32
-    )
-    return product * inv_root
-
-
 def local(hidden, norm_gain, queries, out_grad, kv_inner, kv_outer, momentum):
     inv_root = D ** (-0.5)
-    groups = lax.axis_size("group")
-    rows_in = normed_rows(hidden[0], norm_gain)
+    groups = lax.axis_size(GROUP)
     local_weights = kv_inner[0]
     kv_cols = local_weights.shape[1]
-    projected = jnp.dot(
-        rows_in,
-        lax.all_gather(local_weights, FSDP, axis=0, tiled=True),
-        preferred_element_type=jnp.float32,
-    )
-    kv_rows = (projected * inv_root).astype(jnp.bfloat16)
+    kv_rows, rows_t = gathered_projection(
+        hidden[0].reshape(TOK, D), norm_gain.reshape(1, D), local_weights
+    )
     seq_local = queries.shape[1]
     kv_rows = kv_rows.reshape(seq_local, queries.shape[2], kv_cols)
     kv_grad = kv_grads(queries[0], kv_rows, out_grad[0]).reshape(-1, kv_cols)
-    gradient = scatter_axes(
-        grad_term(rows_in, kv_grad, inv_root).astype(jnp.bfloat16), FSDP, (1, 2, 0), 0
-    ).astype(jnp.float32)
+    product = jnp.dot(rows_t, kv_grad, preferred_element_type=F32) * inv_root
+    gradient = scatter_axes(product.astype(BF), FSDP, (1, 2, 0), 0).astype(F32)
     fresh = local_weights.astype(jnp.float32) - inner_rate * gradient
     coded, scales = quantize(kv_outer - fresh)
-    all_coded, all_scales = side_by_side((coded[None], scales[None]), "group", 0, 2)
+    all_coded, all_scales = side_by_side((coded[None], scales[None]), GROUP, 0, 2)
     totals = jnp.zeros(kv_outer.shape, jnp.float32)
     for member in range(groups):
         totals = totals + dequantize(all_coded[member], all_scales[member])
@@ -160,20 +398,20 @@
 
 def solution(mesh):
     split = Mesh(
-        mesh.devices.reshape(mesh.shape["group"], 2, 4, 4), ("group", "fsdp_0", "fsdp_1", "fsdp_2")
+        mesh.devices.reshape(2, 2, 2, 4, 4), GROUP + FSDP
     )
     return jax.shard_map(
         local,
         mesh=split,
         in_specs=(
-            P("group", FSDP, None, None),
+            P(GROUP, FSDP, None, None),
             P(),
-            P("group", FSDP, None, None),
-            P("group", FSDP, None, None),
-            P("group", FSDP, None),
+            P(GROUP, FSDP, None, None),
+            P(GROUP, FSDP, None, None),
+            P(GROUP, FSDP, None),
             P(FSDP, None),
             P(FSDP, None),
         ),
-        out_specs=(P("group", FSDP, None), P(FSDP, None), P(FSDP, None)),
+        out_specs=(P(GROUP, FSDP, None), P(FSDP, None), P(FSDP, None)),
         check_vma=False,
     )

time: 439 us -> 337 us (0.77)
  waiting for transfers between devices: 305 us -> 159 us
  Pallas kernels: 0 us -> 68.1 us
  other arithmetic: 22.4 us -> 8.21 us
  matrix products: 43.3 us -> 32.9 us
    all_gather x1 -> x0, waiting for transfers between devices: 131 us -> none  [local(): lax.all_gather(local_weights, FSDP, axis=0, tiled=True)]
    pallas_call x0 -> x1, Pallas kernels: none -> 68.1 us  [gathered_projection(): pl.pallas_call(project_kernel, out_shape=(jax.ShapeDtypeStruct((TOK, KVC)...]
    reduce_scatter x3, waiting for transfers between devices: 173 us -> 159 us  [reduced_to_own(): tiles = lax.psum_scatter(tiles, axes[k], scatter_dimension=0, tiled=True)]
    convert_element_type x2 -> x0, other arithmetic: 11.3 us -> none  [normed_rows(): (looked * lax.rsqrt(mean_sq + norm_eps) * norm_gain).astype(jnp.bfloat16)]
    dot_general x2 -> x1, matrix products: 20.9 us -> 10.8 us  [local(): product = jnp.dot(rows_t, kv_grad, preferred_element_type=F32) * inv_root]
    transpose x1 -> x0, local copies, waits for them, and re-layouts: 9.84 us -> none  [reduced_to_own(): tiles = tiles.transpose(*turns, *range(len(axes), tiles.ndim))]
    another operation x0 -> x1, local copies, waits for them, and re-layouts: none -> 9.83 us  [reduced_to_own(): tiles = tiles.reshape(*shape, *tiles.shape[1:])]
    unnamed x36 -> x35, local copies, waits for them, and re-layouts: 16.4 us -> 16.8 us
  transfers between devices with their start and end apart: 4 -> 3, of which waited for: 4 -> 3; matrix products, arithmetic and copies ran while one was open for 5% -> 0% of each run, Pallas kernels for 0% -> 0%
where the time goes in v1:
time: 337 us
  waiting for transfers between devices  159 us (47%)
  Pallas kernels  68.1 us (20%)
  matrix products  32.9 us (10%)
  local copies, waits for them, and re-layouts  29.2 us (9%)
  blocking collectives  24.5 us (7%)
  between operations  14 us (4%)
  other arithmetic  8.21 us (2%)
    reduce_scatter x3, waiting for transfers between devices, reduced_to_own(): tiles = lax.psum_scatter(tiles, axes[k], scatter_dimension=0, tiled=True)  159 us
    pallas_call x1, Pallas kernels, gathered_projection(): pl.pallas_call(project_kernel, out_shape=(jax.ShapeDtypeStruct((TOK, KVC)...  68.1 us
    all_to_all x1, blocking collectives, sent_to_all(): return lax.all_to_all(copies, axis, split_axis=0, concat_axis=0, tiled=True)  24.5 us
    unnamed x35, local copies, waits for them, and re-layouts  16.8 us
    dot_general x2, matrix products, attend(): jnp.einsum('sgrlm,smgd->slgrd', prob_rows, value_h, preferred_element_typ...  13 us
    dot_general x1, matrix products, local(): product = jnp.dot(rows_t, kv_grad, preferred_element_type=F32) * inv_root  10.8 us
    another operation x1, local copies, waits for them, and re-layouts, reduced_to_own(): tiles = tiles.reshape(*shape, *tiles.shape[1:])  9.83 us
    dot_general x2, matrix products, attend(): jnp.einsum('slgrd,smgd->sgrlm', query_h, key_h, preferred_element_type=jn...  9.16 us
  transfers between devices with their start and end apart: 3, of which 3 were waited for; matrix products, arithmetic and copies ran while one was open for 0% of the time, Pallas kernels for 0%

profile of v1, /device:TPU:1, one launch (start us, length us, event | category | flops | bytes accessed | tf_op | source)
XLA Modules:
  0.0 336.7 jit_solution(11642803044128490211)
XLA Ops:
  7.2 0.0 reduce-scatter.4.cloned.1.call-start
  7.2 0.7 iota_compare_fusion
  7.9 3.0 copy.27
  10.9 0.0 copy-start.4
  10.9 0.0 copy-start
  10.9 1.2 copy-done
  12.1 0.0 copy-start.2
  12.1 0.7 copy-done.2
  12.8 68.1 %shard_map.94 = (bf16[512,1024]{1,0:T(8,128)(2,1)S(1)}, bf16[5120,512]{1,0:T(8,128)(2,1)}) custom-call(bf16[512,5120]{1,0:T(8,128)(2,1)} %bitcast.218, f32[1,5120]{1,0:T(1,128)S(1)} %bitcast.209, bf16[160,1024]{1,0:T(8,128)(2,1)S(1)} %bitcast.207), custom_call_target="tpu_custom_call" | custom-call | tf_op jit(solution)/shard_map/pallas_call | solution.py:247
  80.9 0.9 fusion.48
  81.8 2.0 copy.47
  83.9 2.9 fusion.10
  86.7 0.0 copy-done.4
  86.7 0.0 copy-start.3
  86.8 4.0 %copy-done.3 = f32[2,4,256,256,5]{3,2,4,1,0:T(8,128)} copy-done((f32[2,4,256,256,5]{3,2,4,1,0:T(8,128)}, f32[2,4,256,256,5]{3,2,4,1,0:T(8,128)S(1)}, u32[]{:S(2)}) %copy-start.3) | copy-done | bytes 10485784
  90.7 2.6 fusion.12
  93.3 1.0 copy.48
  94.3 0.0 slice-start
  94.3 4.5 %copy.30 = bf16[1,2,256,2560]{2,3,1,0:T(8,128)(2,1)} copy(bf16[1,2,256,2560]{3,2,1,0:T(8,128)(2,1)} %param.10) | data formatting | bytes 5242880 | tf_op args[3]
  98.8 0.0 slice-start.1
  98.8 0.0 slice-start.2
  98.9 0.0 copy-start.8
  98.9 0.0 copy-start.10
  98.9 7.7 %fusion.28 = bf16[2,4,256,128]{2,3,1,0:T(8,128)(2,1)S(1)} fusion(bf16[2,4,128,5,256]{4,2,3,1,0:T(8,128)(2,1)} %bitcast.223, f32[2,4,256,256,5]{3,2,4,1,0:T(8,128)} %copy-done.3, f32[2,4,5,256]{3,2,1,0:T(8,128)S(1)} %fusion.12, f32[2,4,5,256]{3,2,1,0:T(8,128)S(1)} %get-tuple-element.18, pred[256,256]{0,1:T(8,128)(4,1)S(1)} %iota_compare_fusion.1), kind=kOutput, calls=%fused_computation.30 | convolution fusion | flops 684457984 | bytes 13778944 | tf_op jit(solution)/shard_map/transpose(jvp(sgrlm,smgd->slgrd))/dot_general | solution.py:339
  106.6 0.0 slice-done
  106.6 0.0 slice-done.1
  106.6 0.0 slice-done.2
  106.6 0.2 copy-done.8
  106.8 0.0 copy-done.10
  106.8 0.0 copy-start.5
  106.8 5.3 %fusion.7 = (f32[2,4,5,256]{3,2,1,0:T(8,128)S(1)}, bf16[2,4,256,5,256]{4,2,3,1,0:T(8,128)(2,1)}) fusion(f32[2,4,256,256,5]{3,2,4,1,0:T(8,128)S(1)} %bitcast.212, f32[2,4,5,256]{3,2,1,0:T(8,128)S(1)} %multiply_divide_fusion, f32[2,4,5,256]{3,2,1,0:T(8,128)S(1)} %get-tuple-element.18, pred[256,256]{0,1:T(8,128)(4,1)S(1)} %iota_compare_fusion.1, ...), kind=kOutput, calls=%fused_computation.10 | convolution fusion | flops 692049920 | bytes 19062784 | tf_op jit(solution)/shard_map/transpose(jvp(sgrlm,smgd->slgrd))/dot_general | solution.py:339
  112.1 0.0 copy-done.5
  112.1 0.0 copy-done.11
  112.1 6.3 %fusion.25 = bf16[2,4,256,128]{2,3,1,0:T(8,128)(2,1)S(1)} fusion(bf16[2,256,4,5,128]{1,4,3,2,0:T(8,128)(2,1)S(1)} %bitcast.215, bf16[2,4,256,5,256]{4,2,3,1,0:T(8,128)(2,1)} %get-tuple-element.21, f32[2,4,256,256,5]{3,2,4,1,0:T(8,128)S(1)} %bitcast.212, f32[2,4,256,5]{2,3,1,0:T(8,128)S(1)} %bitcast.232, f32[2,4,256,5]{2,3,1,0:T(8,128)S(1)} %negate_bitcast_fusion, ...), kind=kOutput, calls=%fused_computation.29 | convolution fusion | flops 694943744 | bytes 19062784 | tf_op jit(solution)/shard_map/transpose(jvp(slgrd,smgd->sgrlm))/dot_general | solution.py:330
  118.4 0.2 copy.35
  118.6 0.2 copy.32
  118.9 0.1 pad_add_fusion
  119.0 10.8 %multiply_convert_fusion = bf16[5120,1024]{1,0:T(8,128)(2,1)} fusion(bf16[5120,512]{1,0:T(8,128)(2,1)} %get-tuple-element.5, bf16[512,1024]{1,0:T(8,128)(2,1)S(1)} %bitcast.228), kind=kOutput, calls=%fused_computation | convolution fusion | flops 5379194880 | bytes 16777216 | tf_op jit(solution)/shard_map/dot_general | solution.py:385
  129.8 9.8 %copy.36 = bf16[2,4,4,160,1024]{4,3,0,2,1:T(8,128)(2,1)} copy(bf16[2,4,4,160,1024]{4,3,2,1,0:T(8,128)(2,1)} %bitcast.213) | data formatting | bytes 20971520 | tf_op jit(solution)/shard_map/reshape;reshape | solution.py:279
  139.6 0.0 reduce-scatter.4.cloned.1.call-update
  139.7 0.0 copy-start.9
  139.7 0.0 reduce-scatter.6.cloned.1.call-start
  139.7 102.8 %reduce-scatter.4.cloned.1.call-done = bf16[8,160,1024]{2,1,0:T(8,128)(2,1)} async-done(((bf16[32,160,1024]{2,1,0:T(8,128)(2,1)}), bf16[8,160,1024]{2,1,0:T(8,128)(2,1)}) %reduce-scatter.4.cloned.1.call-update) | async-done | bytes 2621456 | tf_op jit(solution)/shard_map/reduce_scatter | solution.py:283
  242.5 0.0 reduce-scatter.6.cloned.1.call-update
  242.5 0.3 reduce-scatter.8.cloned.1.call-start
  242.8 36.1 %reduce-scatter.6.cloned.1.call-done = bf16[2,160,1024]{2,1,0:T(8,128)(2,1)} async-done(((bf16[8,160,1024]{2,1,0:T(8,128)(2,1)}), bf16[2,160,1024]{2,1,0:T(8,128)(2,1)}) %reduce-scatter.6.cloned.1.call-update) | async-done | bytes 655376 | tf_op jit(solution)/shard_map/reduce_scatter | solution.py:283
  278.9 0.0 reduce-scatter.8.cloned.1.call-update
  278.9 20.5 %reduce-scatter.8.cloned.1.call-done = bf16[1,160,1024]{2,1,0:T(8,128)(2,1)} async-done(((bf16[2,160,1024]{2,1,0:T(8,128)(2,1)}), bf16[1,160,1024]{2,1,0:T(8,128)(2,1)}) %reduce-scatter.8.cloned.1.call-update) | async-done | bytes 327696 | tf_op jit(solution)/shard_map/reduce_scatter | solution.py:283
  299.4 0.0 copy-done.1
  299.4 0.0 copy-done.6
  299.4 1.2 abs_bitcast_fusion
  300.6 0.1 copy.49
  300.7 0.2 reduce_max.19
  301.0 0.2 div.49
  301.2 1.3 fusion.36
  302.5 0.1 broadcast_in_dim.47
  302.6 24.5 %all_to_all.5 = bf16[4,1,160,1032]{3,2,1,0:T(8,128)(2,1)S(1)} all-to-all(bf16[4,1,160,1032]{3,2,1,0:T(8,128)(2,1)S(1)} %broadcast_in_dim.47), channel_id=1, replica_groups=mesh['hi'=2,'core'=2,'lo'=2,'x'=4,'z'=4] {'hi','core'}, dimensions={0} | all-to-all | bytes 2641920 | tf_op jit(solution)/shard_map/all_to_all | solution.py:306
  327.2 0.2 mul.138
  327.4 0.2 mul.135
  327.6 0.2 mul.132
  327.9 0.2 mul.129
  328.1 0.0 copy-done.9
  328.1 0.0 copy-done.7
  328.1 2.1 fusion.35
  (11 shorter events, 0.1 us)
Async XLA Ops:
  7.2 235.3 %reduce-scatter.4.cloned.1.call-start = ((), (), s32[]{:S(2)}) async-start(), calls=%async_computation.4 | async-start | bytes 13107200 | tf_op jit(solution)/shard_map/reduce_scatter | solution.py:283
  10.9 75.9 %copy-start.4 = (bf16[1,2,256,2560]{2,3,1,0:T(8,128)(2,1)}, bf16[1,2,256,2560]{2,3,1,0:T(8,128)(2,1)S(1)}, u32[]{:S(2)}) copy-start(bf16[1,2,256,2560]{2,3,1,0:T(8,128)(2,1)S(1)} %copy.27) | copy-start | bytes 7864324
  10.9 1.2 copy-start
  12.1 0.7 copy-start.2
  86.7 4.0 %copy-start.3 = (f32[2,4,256,256,5]{3,2,4,1,0:T(8,128)}, f32[2,4,256,256,5]{3,2,4,1,0:T(8,128)S(1)}, u32[]{:S(2)}) copy-start(f32[2,4,256,256,5]{3,2,4,1,0:T(8,128)S(1)} %get-tuple-element.19) | copy-start | bytes 31457284
  94.3 12.3 %slice-start = ((s8[10485760]{0:T(1024)(128)(4,1)}), s8[2097152]{0:T(1024)(128)(4,1)S(1)}, s32[]{:S(2)}) async-start(s8[10485760]{0:T(1024)(128)(4,1)} %bitcast.211), calls=%async_computation.7 | async-start | bytes 4194304
  98.8 7.7 %slice-start.1 = ((s8[10485760]{0:T(1024)(128)(4,1)}), s8[4194304]{0:T(1024)(128)(4,1)S(1)}, s32[]{:S(2)}) async-start(s8[10485760]{0:T(1024)(128)(4,1)} %bitcast.211), calls=%async_computation.8 | async-start | bytes 8388608
  98.8 7.8 %slice-start.2 = ((s8[10485760]{0:T(1024)(128)(4,1)}), s8[4194304]{0:T(1024)(128)(4,1)S(1)}, s32[]{:S(2)}) async-start(s8[10485760]{0:T(1024)(128)(4,1)} %bitcast.211), calls=%async_computation.9 | async-start | bytes 8388608
  98.9 7.9 %copy-start.8 = (bf16[1,2,256,2560]{2,3,1,0:T(8,128)(2,1)S(1)}, bf16[1,2,256,2560]{2,3,1,0:T(8,128)(2,1)}, u32[]{:S(2)}) copy-start(bf16[1,2,256,2560]{2,3,1,0:T(8,128)(2,1)} %copy.30) | copy-start | bytes 7864324
  98.9 8.0 %copy-start.10 = (bf16[2,256,512]{1,2,0:T(8,128)(2,1)S(1)}, bf16[2,256,512]{1,2,0:T(8,128)(2,1)}, u32[]{:S(2)}) copy-start(bf16[2,256,512]{1,2,0:T(8,128)(2,1)} %copy.48) | copy-start | bytes 1572868
  106.8 5.3 %copy-start.5 = (bf16[1,2,256,2560]{2,3,1,0:T(8,128)(2,1)S(1)}, bf16[1,2,256,2560]{2,3,1,0:T(8,128)(2,1)}, u32[]{:S(2)}) copy-start(bf16[1,2,256,2560]{2,3,1,0:T(8,128)(2,1)} %copy-done.4) | copy-start | bytes 7864324
  106.8 5.3 %copy-start.11 = (pred[256,256]{1,0:T(8,128)(4,1)S(1)}, pred[256,256]{1,0:T(8,128)(4,1)}, u32[]{:S(2)}) copy-start(pred[256,256]{1,0:T(8,128)(4,1)} %iota_compare_fusion) | copy-start | bytes 196612
  139.6 159.8 %copy-start.1 = (bf16[1,160,1024]{2,1,0:T(8,128)(2,1)S(1)}, bf16[1,160,1024]{2,1,0:T(8,128)(2,1)}, u32[]{:S(2)}) copy-start(bf16[1,160,1024]{2,1,0:T(8,128)(2,1)} %param.11) | copy-start | bytes 983044
  139.6 159.8 %copy-start.6 = (f32[160,1024]{1,0:T(8,128)S(1)}, f32[160,1024]{1,0:T(8,128)}, u32[]{:S(2)}) copy-start(f32[160,1024]{1,0:T(8,128)} %param.12) | copy-start | bytes 1966084
  139.7 188.5 %copy-start.9 = (f32[160,1024]{1,0:T(8,128)S(1)}, f32[160,1024]{1,0:T(8,128)}, u32[]{:S(2)}) copy-start(f32[160,1024]{1,0:T(8,128)} %param.13) | copy-start | bytes 1966084
  139.7 139.2 %reduce-scatter.6.cloned.1.call-start = ((), (), s32[]{:S(2)}) async-start(), calls=%async_computation.5 | async-start | bytes 3276800 | tf_op jit(solution)/shard_map/reduce_scatter | solution.py:283
  242.5 56.9 %reduce-scatter.8.cloned.1.call-start = ((), (), s32[]{:S(2)}) async-start(), calls=%async_computation.6 | async-start | bytes 983040 | tf_op jit(solution)/shard_map/reduce_scatter | solution.py:283
  299.4 28.7 %copy-start.7 = (bf16[1,160,1024]{2,1,0:T(8,128)(2,1)S(1)}, bf16[1,160,1024]{2,1,0:T(8,128)(2,1)}, u32[]{:S(2)}) copy-start(bf16[1,160,1024]{2,1,0:T(8,128)(2,1)} %reduce-scatter.8.cloned.1.call-done) | copy-start | bytes 983044
Sparse Core Ops, SparseCore 0:
  139.8 102.6 reduce-scatter.3
  244.9 33.9 reduce-scatter.5
  281.2 18.0 reduce-scatter.7

commit v2 on v1

--- a/solution.py
+++ b/solution.py
@@ -274,126 +274,363 @@
     )(hidden, gain, w)
 
 
-def reduced_to_own(tiles, axes, turns):
-    shape = [lax.axis_size(a) for a in axes]
-    tiles = tiles.reshape(*shape, *tiles.shape[1:])
-    tiles = tiles.transpose(*turns, *range(len(axes), tiles.ndim))
-    tiles = tiles.reshape(-1, *tiles.shape[len(axes) :])
-    for k in turns:
-        tiles = lax.psum_scatter(tiles, axes[k], scatter_dimension=0, tiled=True)
-    return tiles[0]
-
-
-def in_blocks(value, dim, length):
-    shape = value.shape
-    tiles = value.reshape(*shape[:dim], length, shape[dim] // length, *shape[dim + 1 :])
-    return jnp.moveaxis(tiles, dim, 0)
-
-
-def scatter_axes(value, axes, turns, dim):
-    length = lax.axis_size(axes)
-    return reduced_to_own(in_blocks(value, dim, length), axes, turns)
-
-
-def laid_out(tiles, dim):
-    tiles = jnp.moveaxis(tiles, 0, dim)
-    shape = tiles.shape
-    return tiles.reshape(*shape[:dim], shape[dim] * shape[dim + 1], *shape[dim + 2 :])
-
-
-def sent_to_all(value, axis):
-    copies = jnp.broadcast_to(value, (lax.axis_size(axis), *value.shape))
-    return lax.all_to_all(copies, axis, split_axis=0, concat_axis=0, tiled=True)
-
-
-def gather_directly(value, axis, dim):
-    return laid_out(sent_to_all(value, axis), dim)
-
-
-def side_by_side(arrays, axis, dim, along):
-    both = jnp.concatenate(arrays, axis=along)
-    out, at, finished = (gather_directly(both, axis, dim), 0, [])
-    for a in arrays:
-        finished.append(lax.slice_in_dim(out, at, at + a.shape[along], axis=along))
-        at += a.shape[along]
-    return tuple(finished)
-
-
-def attend(queries, kv_rows):
-    seq_count, length, query_width = queries.shape
-    kv_width = kv_rows.shape[-1] // 2
-    kv_heads = kv_width // HD
-    repeat = query_width // (kv_heads * HD)
-    query_h = queries.reshape(seq_count, length, kv_heads, repeat, HD)
-    key_h = kv_rows[..., :kv_width].reshape(seq_count, length, kv_heads, HD)
-    value_h = kv_rows[..., kv_width:].reshape(seq_count, length, kv_heads, HD)
-    scores = jnp.einsum(
-        "slgrd,smgd->sgrlm", query_h, key_h, preferred_element_type=jnp.float32
-    ) * HD ** (-0.5)
-    places = jnp.arange(length)
-    causal = places[None, :] <= places[:, None]
-    scores = jnp.where(causal, scores, -1e30)
-    highest = lax.stop_gradient(jnp.max(scores, axis=-1, keepdims=True))
-    exp_scores = jnp.exp(scores - highest)
-    prob_rows = (exp_scores / jnp.sum(exp_scores, axis=-1, keepdims=True)).astype(jnp.bfloat16)
-    mixed_out = jnp.einsum(
-        "sgrlm,smgd->slgrd", prob_rows, value_h, preferred_element_type=jnp.float32
-    )
-    return mixed_out.reshape(seq_count, length, query_width)
-
-
-def kv_grads(queries, kv_rows, out_grad):
-
-    def loss_part(kv_value):
-        return attend(queries, kv_value)
-
-    _, pullback = jax.vjp(loss_part, kv_rows)
-    return pullback(out_grad.astype(jnp.float32))[0]
-
-
-def quantize(delta):
-    row_count = delta.shape[0]
-    shaped = delta.reshape(row_count, -1, QBLOCK)
-    scales = (jnp.max(jnp.abs(shaped), axis=-1) + scale_eps).astype(jnp.bfloat16)
-    coded = (shaped / scales.astype(jnp.float32)[..., None]).astype(jnp.bfloat16)
-    return (coded.reshape(row_count, -1), scales)
-
-
-def dequantize(coded, scales):
-    row_count = coded.shape[0]
-    shaped = coded.reshape(row_count, scales.shape[1], -1).astype(jnp.float32)
-    return (shaped * scales.astype(jnp.float32)[..., None]).reshape(row_count, -1)
-
-
-def nesterov(outer_rows, moment_rows, average):
-    moment_next = momentum_decay * moment_rows + average
-    outer_next = outer_rows - outer_rate * (momentum_decay * moment_next + average)
-    return (outer_next, moment_next)
+class Scatter:
+    def __init__(self, place, g8, via, near, across, last, send, recv):
+        self.place, self.g8, self.send, self.recv = place, g8, send, recv
+        self.via, self.near, self.across, self.last = via, near, across, last
+
+    def copy(self, p, k):
+        pc, g = self.place, self.g8
+        plus = (p // 2) % 2 == 0
+        src, dst, dev = {
+            0: lambda: (pc.row(g, p, pc.y, 2), self.via.at[p, 0], pc.dev(p, False, 1)),
+            1: lambda: (pc.row(g, p, pc.yo, 2), self.via.at[p, 1], pc.dev(p, False, -1)),
+            2: lambda: (pc.row(g, p, pc.y, 1), self.near.at[p, 0], pc.dev(p, False, 1)),
+            3: lambda: (pc.row(g, p, pc.yo, 1), self.near.at[p, 1], pc.dev(p, False, 1)),
+            4: lambda: (pc.row(g, p, pc.y, -1), self.near.at[p, 2], pc.dev(p, False, -1)),
+            5: lambda: (pc.row(g, p, pc.yo, -1), self.near.at[p, 3], pc.dev(p, False, -1)),
+            6: lambda: (pc.row(g, p, pc.yo, 0), self.across.at[p], {"lo": pc.yo}),
+            7: lambda: (
+                pc.block(g, p, pc.y, 2, 0),
+                self.last.at[p, 2],
+                pc.dev(p, True, 1 if plus else -1),
+            ),
+            8: lambda: (pc.block(g, p, pc.y, 1, 0), self.last.at[p, 0], pc.dev(p, True, 1)),
+            9: lambda: (pc.block(g, p, pc.y, -1, 0), self.last.at[p, 1], pc.dev(p, True, -1)),
+        }[k]()
+        return remote(src, dst, self.send.at[p, k], self.recv.at[p, k], dev)
+
+    def start(self, p, k):
+        self.copy(p, k).start()
+
+    def landed(self, p, k):
+        self.copy(p, k).wait_recv()
+
+    def add(self, dst, *terms):
+        total = dst[...].astype(F32)
+        for t in terms:
+            total = total + t[...].astype(F32)
+        dst[...] = total.astype(BF)
+
+    def add_rows(self, dst, *terms):
+        for i in range(4):
+            self.add(dst.at[i], *[t.at[i] for t in terms])
+
+    def stage(self, p, s):
+        pc, g = self.place, self.g8
+        start, landed = functools.partial(self.start, p), functools.partial(self.landed, p)
+        plus = (p // 2) % 2 == 0
+        if s == 0:
+            for k in (0, 1, 3, 4):
+                start(k)
+        elif s == 1:
+            landed(0)
+            self.add_rows(pc.row(g, p, pc.y, 1), self.via.at[p, 0])
+            start(2)
+            landed(1)
+            self.add_rows(pc.row(g, p, pc.yo, -1), self.via.at[p, 1])
+            start(5)
+        elif s == 2:
+            landed(3)
+            landed(5)
+            self.add_rows(pc.row(g, p, pc.yo, 0), self.near.at[p, 1], self.near.at[p, 3])
+            start(6)
+        elif s == 3:
+            landed(2)
+            landed(4)
+            landed(6)
+            self.add_rows(
+                pc.row(g, p, pc.y, 0), self.near.at[p, 0], self.near.at[p, 2], self.across.at[p]
+            )
+            start(7)
+            start(9 if plus else 8)
+        elif s == 4:
+            landed(7)
+            self.add(pc.block(g, p, pc.y, 1 if plus else -1, 0), self.last.at[p, 2])
+            start(8 if plus else 9)
+
+    def total(self, p):
+        pc, g = self.place, self.g8
+        self.landed(p, 8)
+        self.landed(p, 9)
+        own = pc.block(g, p, pc.y, 0, 0)[...].astype(F32)
+        return own + self.last[p, 0].astype(F32) + self.last[p, 1].astype(F32)
+
+    def drain(self):
+        for p in range(8):
+            for k in range(10):
+                self.copy(p, k).wait_send()
+
+
+class Outer:
+    def __init__(self, w, outer, moment, fresh, coded, scales, mine, send, recv):
+        self.hi, self.core = lax.axis_index("hi"), lax.axis_index("core")
+        self.w, self.outer, self.moment, self.fresh = w, outer, moment, fresh
+        self.coded, self.scales, self.mine = coded, scales, mine
+        self.send, self.recv = send, recv
+
+    def slot(self, flip_hi, flip_core):
+        hi = 1 - self.hi if flip_hi else self.hi
+        core = 1 - self.core if flip_core else self.core
+        return hi * 2 + core
+
+    def copy(self, p, k, arriving):
+        buf = self.scales if p == 8 else self.coded
+        if arriving:
+            s = (self.slot(True, False), self.slot(False, True), self.slot(True, True))[k]
+        else:
+            s = self.slot(k == 2, False)
+        ref = buf.at[s] if p == 8 else buf.at[s, p]
+        dev = {"hi": 1 - self.hi} if k == 0 else {"core": 1 - self.core}
+        return remote(ref, ref, self.send.at[p, k], self.recv.at[p, k], dev)
+
+    def code(self, p, grad):
+        c = piece_cols(p)
+        cols = slice(c, c + 128)
+        fresh = self.w[:, cols].astype(F32) - inner_rate * grad
+        self.fresh[:, cols] = fresh
+        delta = self.outer[:, cols] - fresh
+        scale = (jnp.max(jnp.abs(delta), axis=1, keepdims=True) + scale_eps).astype(BF)
+        scale = scale.astype(F32)
+        self.coded[self.slot(False, False), p] = (delta / scale).astype(BF)
+        lane = lax.broadcasted_iota(jnp.int32, self.mine.shape, 1)
+        self.mine[...] = jnp.where(lane == p, scale, self.mine[...])
+        self.copy(p, 0, False).start()
+        self.copy(p, 1, False).start()
+
+    def send_scales(self):
+        self.scales[self.slot(False, False)] = self.mine[...].astype(BF)
+        self.copy(8, 0, False).start()
+        self.copy(8, 1, False).start()
+
+    def forward(self, p):
+        self.copy(p, 0, True).wait_recv()
+        self.copy(p, 2, False).start()
+
+    def arrived(self, p):
+        self.copy(p, 1, True).wait_recv()
+        self.copy(p, 2, True).wait_recv()
+
+    def finish(self, p, blended, outer_new, moment_new):
+        c = piece_cols(p)
+        cols = slice(c, c + 128)
+        total = jnp.zeros((ROWS, 128), F32)
+        for g in range(4):
+            total = total + self.coded[g, p].astype(F32) * self.scales[g][:, p : p + 1].astype(F32)
+        average = total / 4
+        moment_next = momentum_decay * self.moment[:, cols] + average
+        outer_next = self.outer[:, cols] - outer_rate * (momentum_decay * moment_next + average)
+        moment_new[:, cols] = moment_next
+        outer_new[:, cols] = outer_next
+        blended[:, cols] = (
+            blend_share * self.fresh[:, cols] + (1.0 - blend_share) * outer_next
+        ).astype(BF)
+
+    def drain(self):
+        for p in range(9):
+            for k in range(3):
+                self.copy(p, k, False).wait_send()
+
+
+def dot_nt(a, b):
+    return lax.dot_general(a, b, (((1,), (1,)), ((), ())), preferred_element_type=F32)
+
+
+def attend_back(q, og, kv, kvg, prob, cot, h, s):
+    tok = slice(s * 256, s * 256 + 256)
+    key = kv[tok, h * 128 : h * 128 + 128]
+    val = kv[tok, 512 + h * 128 : 640 + h * 128]
+    root = HD ** (-0.5)
+
+    def one(r, carry):
+        at = pl.multiple_of((h * 5 + r) * 128, 128)
+        for b in range(2):
+            m = 128 * (b + 1)
+            rows = pl.ds(s * 256 + b * 128, 128)
+            qb, gb = q[rows, pl.ds(at, 128)], og[rows, pl.ds(at, 128)]
+            sc = dot_nt(key[:m], qb) * root
+            keys = lax.broadcasted_iota(jnp.int32, (m, 128), 0)
+            places = lax.broadcasted_iota(jnp.int32, (m, 128), 1) + b * 128
+            sc = jnp.where(keys <= places, sc, -1e30)
+            ex = jnp.exp(sc - jnp.max(sc, axis=0, keepdims=True))
+            pr = ex * (1.0 / jnp.sum(ex, axis=0, keepdims=True))
+            dp = dot_nt(val[:m], gb).astype(BF).astype(F32)
+            prod = pr * dp
+            ds = prod - pr * jnp.sum(prod, axis=0, keepdims=True)
+            to = pl.ds(pl.multiple_of(r * 256 + b * 128, 128), 128)
+            prob[:m, to] = pr.astype(BF)
+            cot[:m, to] = ds.astype(BF)
+        return carry
+
+    lax.fori_loop(0, 5, one, 0, unroll=UNROLL)
+    base = h * 640
+    rows = slice(s * 256, s * 256 + 256)
+    stack = lambda ref: jnp.concatenate(
+        [ref[rows, base + r * 128 : base + r * 128 + 128] for r in range(5)], axis=0
+    )
+    dk = jnp.dot(cot[...], stack(q), preferred_element_type=F32) * root
+    dv = jnp.dot(prob[...], stack(og), preferred_element_type=F32)
+    kvg[h, tok, :128] = dk.astype(BF)
+    kvg[h, tok, 128:] = dv.astype(BF)
+
+
+UNROLL = 5
+
+
+def grad_rows(rows_t, kvg, g8, h, first, count):
+    inv_root = D ** (-0.5)
+
+    def step(j, carry):
+        j = j + first
+        at = pl.multiple_of(j * 640, 640)
+        out = jnp.dot(rows_t[pl.ds(at, 640), :], kvg[h], preferred_element_type=F32) * inv_root
+        out = out.astype(BF)
+        y, x = j // 4, lax.rem(j, 4)
+        g8[2 * h, y, x] = out[:, :128].reshape(4, ROWS, 128)
+        g8[2 * h + 1, y, x] = out[:, 128:].reshape(4, ROWS, 128)
+        return carry
+
+    lax.fori_loop(0, count, step, 0)
+
+
+def sync_kernel(
+    q_any, og_any, kv, rows_any, w, outer, moment, blended, outer_new, moment_new,
+    q, og, rows_t, kvg, prob, cot, g8, via, near, across, last, fresh, coded, scales, mine,
+    send, recv, x_send, x_recv, load_sem,
+):
+    pc = Place()
+    sc = Scatter(pc, g8, via, near, across, last, send, recv)
+    ex = Outer(w, outer, moment, fresh, coded, scales, mine, x_send, x_recv)
+    loads = [
+        pltpu.make_async_copy(a, b, load_sem.at[i])
+        for i, (a, b) in enumerate(((q_any, q), (og_any, og), (rows_any, rows_t)))
+    ]
+    for cp in loads:
+        cp.start()
+    prob[...] = jnp.zeros_like(prob)
+    cot[...] = jnp.zeros_like(cot)
+    mine[...] = jnp.zeros_like(mine)
+    meet(
+        [{"lo": pc.yo}, {"hi": 1 - ex.hi}, {"core": 1 - ex.core}]
+        + [pc.dev(p, True, o) for p in range(2) for o in (1, -1)]
+    )
+    loads[0].wait()
+    loads[1].wait()
+
+    def stage(s, h):
+        for e in range(2):
+            p = 2 * h + e
+            if s < 5:
+                sc.stage(p, s)
+            elif s == 5:
+                ex.code(p, sc.total(p))
+            else:
+                ex.forward(p)
+
+    def attn(h, s):
+        attend_back(q, og, kv, kvg, prob, cot, h, s)
+
+    def grads(h):
+        grad_rows(rows_t, kvg, g8, h, 0, 8)
+
+    attn(0, 0)
+    attn(0, 1)
+    loads[2].wait()
+    grads(0)
+    stage(0, 0)
+    attn(1, 0)
+    stage(1, 0)
+    attn(1, 1)
+    grads(1)
+    stage(0, 1)
+    stage(2, 0)
+    attn(2, 0)
+    stage(1, 1)
+    stage(3, 0)
+    attn(2, 1)
+    grads(2)
+    stage(0, 2)
+    stage(4, 0)
+    stage(2, 1)
+    attn(3, 0)
+    stage(1, 2)
+    stage(5, 0)
+    stage(3, 1)
+    attn(3, 1)
+    grads(3)
+    stage(0, 3)
+    stage(6, 0)
+    stage(4, 1)
+    stage(2, 2)
+    stage(1, 3)
+    stage(5, 1)
+    stage(3, 2)
+    stage(6, 1)
+    stage(4, 2)
+    stage(2, 3)
+    stage(5, 2)
+    stage(3, 3)
+    stage(6, 2)
+    stage(4, 3)
+    stage(5, 3)
+    ex.send_scales()
+    stage(6, 3)
+    ex.forward(8)
+    for p in range(8):
+        ex.arrived(p)
+    ex.arrived(8)
+    for p in range(8):
+        ex.finish(p, blended, outer_new, moment_new)
+    sc.drain()
+    ex.drain()
+
+
+def synced(q, og, kv, rows_t, w, outer, moment):
+    vm, hbm = pl.BlockSpec(memory_space=pltpu.VMEM), pl.BlockSpec(memory_space=pl.ANY)
+    return pl.pallas_call(
+        sync_kernel,
+        out_shape=(
+            jax.ShapeDtypeStruct((ROWS, KVC), BF),
+            jax.ShapeDtypeStruct((ROWS, KVC), F32),
+            jax.ShapeDtypeStruct((ROWS, KVC), F32),
+        ),
+        in_specs=[hbm, hbm, vm, hbm, vm, vm, vm],
+        out_specs=(vm, vm, vm),
+        scratch_shapes=[
+            pltpu.VMEM((TOK, 2560), BF),
+            pltpu.VMEM((TOK, 2560), BF),
+            pltpu.VMEM((D, TOK), BF),
+            pltpu.VMEM((4, TOK, 256), BF),
+            pltpu.VMEM((256, 1280), BF),
+            pltpu.VMEM((256, 1280), BF),
+            pltpu.VMEM((8, 2, 4, 4, ROWS, 128), BF),
+            pltpu.VMEM((8, 2, 4, ROWS, 128), BF),
+            pltpu.VMEM((8, 4, 4, ROWS, 128), BF),
+            pltpu.VMEM((8, 4, ROWS, 128), BF),
+            pltpu.VMEM((8, 3, ROWS, 128), BF),
+            pltpu.VMEM((ROWS, KVC), F32),
+            pltpu.VMEM((4, 8, ROWS, 128), BF),
+            pltpu.VMEM((4, ROWS, 128), BF),
+            pltpu.VMEM((ROWS, 128), F32),
+            pltpu.SemaphoreType.DMA((8, 10)),
+            pltpu.SemaphoreType.DMA((8, 10)),
+            pltpu.SemaphoreType.DMA((9, 3)),
+            pltpu.SemaphoreType.DMA((9, 3)),
+            pltpu.SemaphoreType.DMA((3,)),
+        ],
+        compiler_params=pltpu.CompilerParams(
+            collective_id=1, has_side_effects=True, vmem_limit_bytes=60 * 1024 * 1024
+        ),
+    )(q, og, kv, rows_t, w, outer, moment)
 
 
 def local(hidden, norm_gain, queries, out_grad, kv_inner, kv_outer, momentum):
-    inv_root = D ** (-0.5)
-    groups = lax.axis_size(GROUP)
-    local_weights = kv_inner[0]
-    kv_cols = local_weights.shape[1]
-    kv_rows, rows_t = gathered_projection(
-        hidden[0].reshape(TOK, D), norm_gain.reshape(1, D), local_weights
-    )
-    seq_local = queries.shape[1]
-    kv_rows = kv_rows.reshape(seq_local, queries.shape[2], kv_cols)
-    kv_grad = kv_grads(queries[0], kv_rows, out_grad[0]).reshape(-1, kv_cols)
-    product = jnp.dot(rows_t, kv_grad, preferred_element_type=F32) * inv_root
-    gradient = scatter_axes(product.astype(BF), FSDP, (1, 2, 0), 0).astype(F32)
-    fresh = local_weights.astype(jnp.float32) - inner_rate * gradient
-    coded, scales = quantize(kv_outer - fresh)
-    all_coded, all_scales = side_by_side((coded[None], scales[None]), GROUP, 0, 2)
-    totals = jnp.zeros(kv_outer.shape, jnp.float32)
-    for member in range(groups):
-        totals = totals + dequantize(all_coded[member], all_scales[member])
-    average = totals / groups
-    outer_new, momentum_new = nesterov(kv_outer, momentum, average)
-    blended = (blend_share * fresh + (1.0 - blend_share) * outer_new).astype(jnp.bfloat16)
-    return (blended[None], outer_new, momentum_new)
+    own = kv_inner[0]
+    kv, rows_t = gathered_projection(hidden[0].reshape(TOK, D), norm_gain.reshape(1, D), own)
+    blended, outer_new, moment_new = synced(
+        queries[0].reshape(TOK, -1), out_grad[0].reshape(TOK, -1), kv, rows_t, own, kv_outer, momentum
+    )
+    return (blended[None], outer_new, moment_new)
 
 
 def solution(mesh):

time: 337 us -> 167 us (0.50)
  waiting for transfers between devices: 159 us -> 0 us
  Pallas kernels: 68.1 us -> 157 us
  matrix products: 32.9 us -> 0 us
  blocking collectives: 24.5 us -> 0 us
  local copies, waits for them, and re-layouts: 29.2 us -> 8.39 us
  between operations: 14 us -> 0.67 us
  other arithmetic: 8.21 us -> 0 us
    reduce_scatter x3 -> x0, waiting for transfers between devices: 159 us -> none  [reduced_to_own(): tiles = lax.psum_scatter(tiles, axes[k], scatter_dimension=0, tiled=True)]
    pallas_call x0 -> x1, Pallas kernels: none -> 89.4 us  [synced(): pl.pallas_call(sync_kernel, out_shape=(jax.ShapeDtypeStruct((ROWS, KVC),...]
    dot_general x5 -> x0, matrix products: 32.9 us -> none  [the longest x2 13 us: attend(): jnp.einsum('sgrlm,smgd->slgrd', prob_rows, value_h, preferred_element_typ...]
    all_to_all x1 -> x0, blocking collectives: 24.5 us -> none  [sent_to_all(): return lax.all_to_all(copies, axis, split_axis=0, concat_axis=0, tiled=True)]
    another operation x1 -> x0, local copies, waits for them, and re-layouts: 9.83 us -> none  [reduced_to_own(): tiles = tiles.reshape(*shape, *tiles.shape[1:])]
    unnamed x35 -> x9, local copies, waits for them, and re-layouts: 16.8 us -> 8.39 us
  transfers between devices with their start and end apart: 3 -> 0, of which waited for: 3 -> 0; matrix products, arithmetic and copies ran while one was open for 0% -> 0% of each run, Pallas kernels for 0% -> 0%
where the time goes in v2:
time: 167 us; the launch traced here: 166 us
  Pallas kernels  157 us (94%)
  local copies, waits for them, and re-layouts  8.39 us (5%)
    pallas_call x1, Pallas kernels, synced(): pl.pallas_call(sync_kernel, out_shape=(jax.ShapeDtypeStruct((ROWS, KVC),...  89.4 us
    pallas_call x1, Pallas kernels, gathered_projection(): pl.pallas_call(project_kernel, out_shape=(jax.ShapeDtypeStruct((TOK, KVC)...  68 us
    unnamed x9, local copies, waits for them, and re-layouts  8.39 us

profile of v2, /device:TPU:1, one launch (start us, length us, event | category | flops | bytes accessed | tf_op | source)
XLA Modules:
  0.0 166.5 jit_solution(15111436444718233518)
XLA Ops:
  0.6 0.0 copy-start
  0.6 1.0 copy-done
  1.6 0.0 copy-start.2
  1.6 0.7 copy-done.2
  2.3 68.0 %shard_map.94 = (bf16[512,1024]{1,0:T(8,128)(2,1)S(1)}, bf16[5120,512]{1,0:T(8,128)(2,1)}) custom-call(bf16[512,5120]{1,0:T(8,128)(2,1)} %bitcast.9, f32[1,5120]{1,0:T(1,128)S(1)} %bitcast.8, bf16[160,1024]{1,0:T(8,128)(2,1)S(1)} %bitcast.7), custom_call_target="tpu_custom_call" | custom-call | tf_op jit(solution)/shard_map/pallas_call | solution.py:247
  70.4 0.0 copy-start.1
  70.4 1.0 copy-done.1
  71.4 89.4 %shard_map.95 = (bf16[160,1024]{1,0:T(8,128)(2,1)}, f32[160,1024]{1,0:T(8,128)}, f32[160,1024]{1,0:T(8,128)}) custom-call(bf16[512,2560]{1,0:T(8,128)(2,1)} %bitcast.10, bf16[512,2560]{1,0:T(8,128)(2,1)} %bitcast.11, bf16[512,1024]{1,0:T(8,128)(2,1)} %copy-done.1, bf16[5120,512]{1,0:T(8,128)(2,1)} %get-tuple-element.9.rows_any, bf16[160,1024]{1,0:T(8,128)(2,1)} %bitcast.6, ...), custom_call_target="tpu_custom_call" | custom-call | tf_op jit(solution)/shard_map/pallas_call | solution.py:590
  160.8 1.7 %copy.13 = bf16[1,160,1024]{2,1,0:T(8,128)(2,1)} copy(bf16[1,160,1024]{2,1,0:T(8,128)(2,1)} %bitcast.12) | data formatting | bytes 655360
  162.5 2.0 %copy.14 = f32[160,1024]{1,0:T(8,128)} copy(f32[160,1024]{1,0:T(8,128)} %get-tuple-element.17) | data formatting | bytes 1310720
  164.5 2.0 %copy.15 = f32[160,1024]{1,0:T(8,128)} copy(f32[160,1024]{1,0:T(8,128)} %get-tuple-element.18) | data formatting | bytes 1310720
Async XLA Ops:
  0.6 1.0 copy-start
  1.6 0.7 copy-start.2
  70.4 1.0 copy-start.1

commit v3 on v2

v3 whole, which is shorter than its diff:
```python
import functools
import jax
import jax.numpy as jnp
from jax import lax
from jax.experimental import pallas as pl
from jax.experimental.pallas import tpu as pltpu
from jax.sharding import Mesh
from jax.sharding import PartitionSpec as P

D = 5120
HD = 128
KVC = 1024
TOK = 512
ROWS = 160
QBLOCK = 128
GROUP = ("hi", "core")
FSDP = ("lo", "x", "z")
MESH = pl.DeviceIdType.MESH
BF = jnp.bfloat16
F32 = jnp.float32


inner_rate = 0.25
outer_rate = 0.7
momentum_decay = 0.9
blend_share = 0.5
norm_eps = 1e-06
scale_eps = 1e-06


def piece_cols(p):
    return (p // 2) * 128 + (p % 2) * 512


class Place:
    def __init__(self):
        self.y = lax.axis_index("lo")
        self.x = lax.axis_index("x")
        self.z = lax.axis_index("z")
        self.yo = 1 - self.y

    def names(self, p):
        return ("x", "z") if p % 2 == 0 else ("z", "x")

    def at(self, p, first, off):
        v = getattr(self, self.names(p)[0 if first else 1])
        return lax.rem(v + (off + 4), 4)

    def dev(self, p, first, off):
        return {self.names(p)[0 if first else 1]: self.at(p, first, off)}

    def plane(self, q):
        return self.yo if q else self.y

    def half(self, ref, p, q, c_off, h):
        c = self.at(p, False, c_off)
        low = 2 * (self.at(p, True, 0) // 2)
        two = pl.ds(2 - low if h else low, 2)
        if p % 2 == 0:
            return ref.at[p, self.plane(q), two, c]
        return ref.at[p, self.plane(q), c, two]

    def block(self, ref, p, a_off):
        a, c = self.at(p, True, a_off), self.at(p, False, 0)
        if p % 2 == 0:
            return ref.at[p, self.y, a, c]
        return ref.at[p, self.y, c, a]


def remote(src, dst, send, recv, dev):
    return pltpu.make_async_remote_copy(
        src_ref=src, dst_ref=dst, send_sem=send, recv_sem=recv, device_id=dev, device_id_type=MESH
    )


def meet(devs):
    barrier = pltpu.get_barrier_semaphore()
    for dev in devs:
        pl.semaphore_signal(barrier, inc=1, device_id=dev, device_id_type=MESH)
    pl.semaphore_wait(barrier, len(devs))


def up(p):
    return 1 if (p // 2) % 2 == 0 else -1


class Moves:
    def __init__(self, place, send, recv):
        self.place, self.send, self.recv, self.used = place, send, recv, []

    def copy(self, p, k):
        src, dst, dev = self.ends(p, k)
        return remote(src, dst, self.send.at[p, k], self.recv.at[p, k], dev)

    def start(self, p, *keys):
        for k in keys:
            self.copy(p, k).start()
            self.used.append((p, k))

    def landed(self, p, *keys):
        for k in keys:
            self.copy(p, k).wait_recv()

    def drain(self):
        for p, k in self.used:
            self.copy(p, k).wait_send()


class Gather(Moves):
    def __init__(self, place, w8, send, recv):
        super().__init__(place, send, recv)
        self.w8 = w8

    def ends(self, p, k):
        pc, w = self.place, self.w8
        if k < 3:
            src = pc.block(w, p, (0, 0, -up(p))[k])
            return src, src, pc.dev(p, True, (1, -1, up(p))[k])
        if p in LATE_Y:
            if k < 5:
                h = k - 3
                src, dev = pc.half(w, p, 0, 1 if h else -1, h), pc.dev(p, False, -1 if h else 1)
            elif k < 9:
                d, h = (k - 5) // 2, (k - 5) % 2
                src, dev = pc.half(w, p, 0, 0, h), pc.dev(p, False, -1 if d else 1)
            else:
                c, h = (k - 9) // 2, (k - 9) % 2
                src, dev = pc.half(w, p, 0, (0, -1, 1, 2)[c], h), {"lo": pc.yo}
        elif k < 5:
            src, dev = pc.half(w, p, 0, 0, k - 3), {"lo": pc.yo}
        elif k < 13:
            d, q, h = (k - 5) // 4, (k - 5) // 2 % 2, (k - 5) % 2
            src, dev = pc.half(w, p, q, 0, h), pc.dev(p, False, -1 if d else 1)
        else:
            q, h = (k - 13) // 2, (k - 13) % 2
            src, dev = pc.half(w, p, q, 1 if h else -1, h), pc.dev(p, False, -1 if h else 1)
        return src, src, dev

    def act(self, p, s):
        if p in LATE_Y:
            waits, starts = {
                0: ((), (0, 1)),
                1: ((0, 1), (2, 5, 7, 9)),
                2: ((2,), (8, 6, 10)),
                3: ((5,), (3, 11)),
                4: ((8,), (4, 14)),
                5: ((7,), (13,)),
                6: ((6,), (12,)),
                7: ((3,), (15,)),
                8: ((4,), (16,)),
                9: (tuple(range(9, 17)), ()),
            }[s]
        else:
            waits, starts = {
                0: ((), (0, 1)),
                1: ((0, 1), (2, 3, 5, 9)),
                2: ((2,), (4, 10, 6)),
                3: ((3,), (7, 11)),
                4: ((4,), (12, 8)),
                5: ((5,), (13,)),
                6: ((10,), (14,)),
                7: ((7,), (15,)),
                8: ((12,), (16,)),
                9: ((9, 6, 11, 8, 13, 14, 15, 16), ()),
            }[s]
        self.landed(p, *waits)
        self.start(p, *starts)


def norm_rows(rows, gain, start, count):
    def step(i, carry):
        at = pl.ds(pl.multiple_of(start + i * 16, 16), 16)
        looked = rows[at, :].astype(F32)
        mean_sq = jnp.mean(looked * looked, axis=-1, keepdims=True)
        looked = rows[at, :].astype(F32)
        rows[at, :] = (looked * lax.rsqrt(mean_sq + norm_eps) * gain[...]).astype(BF)
        return carry

    lax.fori_loop(0, count // 16, step, 0)


def turn_rows(rows, rows_t, start, count):
    def step(j, carry):
        at = pl.multiple_of((start + j) * 128, 128)
        rows_t[pl.ds(at, 128), :] = rows[:, pl.ds(at, 128)].T
        return carry

    lax.fori_loop(0, count, step, 0)


def project(rows, w8, acc, kv, h):
    inv_root = D ** (-0.5)

    def step(i, carry):
        at = pl.multiple_of(i * 1280, 1280)
        y, x = i // 2, 2 * lax.rem(i, 2)
        pair = [w8[2 * h + e, y, pl.ds(x, 2)].reshape(1280, 128) for e in range(2)]
        acc[...] += jnp.dot(
            rows[:, pl.ds(at, 1280)],
            jnp.concatenate(pair, axis=1),
            preferred_element_type=F32,
        )
        return carry

    acc[...] = jnp.zeros_like(acc)
    lax.fori_loop(0, 4, step, 0)
    out = (acc[...] * inv_root).astype(BF)
    kv[:, h * 128 : h * 128 + 128] = out[:, :128]
    kv[:, 512 + h * 128 : 640 + h * 128] = out[:, 128:]


def interleave(comm, work):
    n = len(comm)
    done = 0
    for i, f in enumerate(comm):
        f()
        upto = (i + 1) * len(work) // n
        for g in work[done:upto]:
            g()
        done = upto


class Scatter(Moves):
    def __init__(self, place, g8, via, near, across, last, send, recv):
        super().__init__(place, send, recv)
        self.g8 = g8
        self.via, self.near, self.across, self.last = via, near, across, last

    def ends(self, p, k):
        pc, g = self.place, self.g8
        if k < 4:
            q, h = k // 2, k % 2
            return pc.half(g, p, q, 2, h), self.via.at[p, k], pc.dev(p, False, -1 if h else 1)
        if k < 12:
            d, q, h = (k - 4) // 4, (k - 4) // 2 % 2, (k - 4) % 2
            off = -1 if d else 1
            return pc.half(g, p, q, off, h), self.near.at[p, k - 4], pc.dev(p, False, off)
        if k < 14:
            return pc.half(g, p, 1, 0, k - 12), self.across.at[p, k - 12], {"lo": pc.yo}
        block = pc.block(g, p, (2, 1, -1)[k - 14])
        return block, self.last.at[p, k - 14], pc.dev(p, True, (up(p), 1, -1)[k - 14])

    def add(self, dst, *terms):
        total = dst[...].astype(F32)
        for t in terms:
            total = total + t[...].astype(F32)
        dst[...] = total.astype(BF)

    def add_half(self, dst, *terms):
        for i in range(2):
            self.add(dst.at[i], *[t.at[i] for t in terms])

    def act(self, p, s):
        pc, g, via, near = self.place, self.g8, self.via, self.near
        if s == 0:
            self.start(p, 3, 2, 7, 10)
        elif s == 1:
            self.start(p, 1, 0, 5, 8)
        elif s in (2, 3, 6, 7):
            q, h = (1 if s < 4 else 0), 1 - s % 2
            self.landed(p, 2 * q + h)
            self.add_half(pc.half(g, p, q, -1 if h else 1, h), via.at[p, 2 * q + h])
            self.start(p, 4 + h * 4 + q * 2 + h)
        elif s in (4, 5):
            h = 5 - s
            self.landed(p, 6 + h, 10 + h)
            self.add_half(pc.half(g, p, 1, 0, h), near.at[p, 2 + h], near.at[p, 6 + h])
            self.start(p, 12 + h)
        elif s in (8, 9):
            h = 9 - s
            self.landed(p, 4 + h, 8 + h, 12 + h)
            self.add_half(
                pc.half(g, p, 0, 0, h), near.at[p, h], near.at[p, 4 + h], self.across.at[p, h]
            )
            self.start(p, 14 if s == 8 else (16 if up(p) > 0 else 15))
        elif s == 10:
            self.landed(p, 14)
            self.add(pc.block(g, p, up(p)), self.last.at[p, 0])
            self.start(p, 15 if up(p) > 0 else 16)

    def total(self, p):
        self.landed(p, 15, 16)
        own = self.place.block(self.g8, p, 0)[...].astype(F32)
        return own + self.last[p, 1].astype(F32) + self.last[p, 2].astype(F32)


class Outer:
    def __init__(self, w, outer, fresh, coded, scales, mine, send, recv):
        self.hi, self.core = lax.axis_index("hi"), lax.axis_index("core")
        self.w, self.outer, self.fresh = w, outer, fresh
        self.coded, self.scales, self.mine = coded, scales, mine
        self.send, self.recv = send, recv

    def slot(self, flip_hi, flip_core):
        hi = 1 - self.hi if flip_hi else self.hi
        core = 1 - self.core if flip_core else self.core
        return hi * 2 + core

    def copy(self, p, k, arriving):
        buf = self.scales if p == 8 else self.coded
        if arriving:
            s = (self.slot(True, False), self.slot(False, True), self.slot(True, True))[k]
        else:
            s = self.slot(k == 2, False)
        ref = buf.at[s] if p == 8 else buf.at[s, p]
        dev = {"hi": 1 - self.hi} if k == 0 else {"core": 1 - self.core}
        return remote(ref, ref, self.send.at[p, k], self.recv.at[p, k], dev)

    def code(self, p, grad):
        c = piece_cols(p)
        cols = slice(c, c + 128)
        fresh = self.w[:, cols].astype(F32) - inner_rate * grad
        self.fresh[:, cols] = fresh
        delta = self.outer[:, cols] - fresh
        scale = (jnp.max(jnp.abs(delta), axis=1, keepdims=True) + scale_eps).astype(BF)
        scale = scale.astype(F32)
        self.coded[self.slot(False, False), p] = (delta / scale).astype(BF)
        lane = lax.broadcasted_iota(jnp.int32, self.mine.shape, 1)
        self.mine[...] = jnp.where(lane == p, scale, self.mine[...])
        self.copy(p, 0, False).start()
        self.copy(p, 1, False).start()

    def send_scales(self):
        self.scales[self.slot(False, False)] = self.mine[...].astype(BF)
        self.copy(8, 0, False).start()
        self.copy(8, 1, False).start()

    def forward(self, p):
        self.copy(p, 0, True).wait_recv()
        self.copy(p, 2, False).start()

    def arrived(self, p):
        self.copy(p, 1, True).wait_recv()
        self.copy(p, 2, True).wait_recv()

    def finish(self, p, average):
        c = piece_cols(p)
        total = jnp.zeros((ROWS, 128), F32)
        for g in range(4):
            total = total + self.coded[g, p].astype(F32) * self.scales[g][:, p : p + 1].astype(F32)
        average[:, c : c + 128] = total / 4

    def drain(self):
        for p in range(9):
            for k in range(3):
                self.copy(p, k, False).wait_send()


def dot_nt(a, b):
    return lax.dot_general(a, b, (((1,), (1,)), ((), ())), preferred_element_type=F32)


def attend_back(q, og, kv, kvg, prob, cot, h, s):
    tok = slice(s * 256, s * 256 + 256)
    key = kv[tok, h * 128 : h * 128 + 128]
    val = kv[tok, 512 + h * 128 : 640 + h * 128]
    root = HD ** (-0.5)

    def one(r, carry):
        at = pl.multiple_of((h * 5 + r) * 128, 128)
        for b in range(2):
            m = 128 * (b + 1)
            rows = pl.ds(s * 256 + b * 128, 128)
            qb, gb = q[rows, pl.ds(at, 128)], og[rows, pl.ds(at, 128)]
            sc = dot_nt(key[:m], qb) * root
            keys = lax.broadcasted_iota(jnp.int32, (m, 128), 0)
            places = lax.broadcasted_iota(jnp.int32, (m, 128), 1) + b * 128
            sc = jnp.where(keys <= places, sc, -1e30)
            ex = jnp.exp(sc - jnp.max(sc, axis=0, keepdims=True))
            pr = ex * (1.0 / jnp.sum(ex, axis=0, keepdims=True))
            dp = dot_nt(val[:m], gb).astype(BF).astype(F32)
            prod = pr * dp
            ds = prod - pr * jnp.sum(prod, axis=0, keepdims=True)
            to = pl.ds(pl.multiple_of(r * 256 + b * 128, 128), 128)
            prob[:m, to] = pr.astype(BF)
            cot[:m, to] = ds.astype(BF)
        return carry

    lax.fori_loop(0, 5, one, 0, unroll=UNROLL)
    base = h * 640
    rows = slice(s * 256, s * 256 + 256)
    stack = lambda ref: jnp.concatenate(
        [ref[rows, base + r * 128 : base + r * 128 + 128] for r in range(5)], axis=0
    )
    dk = jnp.dot(cot[...], stack(q), preferred_element_type=F32) * root
    dv = jnp.dot(prob[...], stack(og), preferred_element_type=F32)
    kvg[h, tok, :128] = dk.astype(BF)
    kvg[h, tok, 128:] = dv.astype(BF)


UNROLL = 5


def grad_rows(rows_t, kvg, g8, h, y):
    inv_root = D ** (-0.5)

    def one(x, carry):
        at = pl.multiple_of((y * 4 + x) * 640, 640)
        out = jnp.dot(rows_t[pl.ds(at, 640), :], kvg[h], preferred_element_type=F32) * inv_root
        out = out.astype(BF)
        g8[2 * h, y, x] = out[:, :128].reshape(4, ROWS, 128)
        g8[2 * h + 1, y, x] = out[:, 128:].reshape(4, ROWS, 128)
        return carry

    lax.fori_loop(0, 4, one, 0)


def step_kernel(
    hidden, gain_any, w_any, q_any, og_any, outer_any,
    fresh, average,
    gain, w, outer, q, og, rows, rows_t, w8, acc, kv, kvg, prob, cot,
    g8, via, near, across, last, coded, scales, mine,
    ag_send, ag_recv, send, recv, x_send, x_recv, load_sem, own_sem, arg_sem,
):
    pc = Place()
    ga = Gather(pc, w8, ag_send, ag_recv)
    sc = Scatter(pc, g8, via, near, across, last, send, recv)
    ex = Outer(w, outer, fresh, coded, scales, mine, x_send, x_recv)
    owns = []
    for p in range(8):
        c = piece_cols(p)
        owns.append(
            pltpu.make_async_copy(
                w_any.at[:, c : c + 128], pc.block(w8, p, 0), own_sem.at[p]
            )
        )
    loads = []
    for i in range(8):
        at = slice(i * 64, i * 64 + 64)
        loads.append(pltpu.make_async_copy(hidden.at[at], rows.at[at], load_sem.at[i]))
    args = [
        pltpu.make_async_copy(a, b, arg_sem.at[i])
        for i, (a, b) in enumerate(
            (
                (gain_any, gain),
                (q_any, q),
                (og_any, og),
                (w_any, w),
                (outer_any, outer),
            )
        )
    ]
    for cp in owns + args[:1] + loads + args[1:]:
        cp.start()
    meet(
        [{"lo": pc.yo}, {"hi": 1 - ex.hi}, {"core": 1 - ex.core}]
        + [pc.dev(p, True, o) for p in range(2) for o in (1, -1)]
    )
    for p in range(8):
        owns[p].wait()
    args[0].wait()

    def norm(i):
        loads[i].wait()
        norm_rows(rows, gain, i * 64, 64)

    def turn(i):
        turn_rows(rows, rows_t, i * 5, 5)

    def scatter(p, s):
        if s < 11:
            sc.act(p, s)
        elif s == 11:
            ex.code(p, sc.total(p))
        else:
            ex.forward(p)

    def attn(h, s):
        attend_back(q, og, kv, kvg, prob, cot, h, s)

    def grads(h, near):
        grad_rows(rows_t, kvg, g8, h, pc.plane(1 - near))

    def proj(h):
        project(rows, w8, acc, kv, h)

    def clear():
        prob[...] = jnp.zeros_like(prob)
        cot[...] = jnp.zeros_like(cot)
        mine[...] = jnp.zeros_like(mine)
        for cp in args[1:]:
            cp.wait()

    acts = dict(G=ga.act, T=scatter, A=attn, M=grads, P=proj, N=norm, U=turn, C=clear)
    for kind, *nums in ORDER:
        acts[kind](*nums)
    ex.send_scales()
    ex.forward(8)
    for p in range(8):
        ex.arrived(p)
    ex.arrived(8)
    for p in range(8):
        ex.finish(p, average)
    ga.drain()
    sc.drain()
    ex.drain()


LATE_Y = (4, 5)

ORDER = (
    ("G", 0, 0), ("G", 1, 0), ("G", 2, 0), ("G", 3, 0), ("G", 4, 0), ("G", 5, 0), ("G", 6, 0),
    ("G", 7, 0), ("N", 0), ("N", 1), ("N", 2), ("G", 0, 1), ("G", 1, 1), ("G", 2, 1), ("G", 3, 1),
    ("N", 3), ("N", 4), ("G", 0, 2), ("N", 5), ("G", 0, 5), ("G", 0, 3), ("N", 6), ("G", 1, 5),
    ("G", 1, 2), ("N", 7), ("G", 1, 3), ("G", 2, 5), ("G", 3, 5), ("U", 0), ("G", 2, 2), ("U", 1),
    ("U", 2), ("G", 0, 6), ("G", 3, 2), ("U", 3), ("G", 1, 6), ("G", 2, 3), ("U", 4), ("G", 3, 3),
    ("U", 5), ("U", 6), ("G", 0, 4), ("G", 7, 1), ("U", 7), ("C",), ("G", 2, 6), ("G", 3, 6),
    ("G", 0, 7), ("G", 1, 7), ("G", 6, 1), ("G", 1, 4), ("G", 2, 4), ("G", 3, 4), ("G", 0, 8),
    ("G", 2, 7), ("G", 3, 7), ("G", 6, 3), ("G", 7, 5), ("G", 6, 2), ("G", 7, 3), ("G", 1, 8),
    ("G", 6, 5), ("G", 2, 8), ("G", 7, 2), ("G", 3, 8), ("G", 6, 4), ("G", 0, 9), ("G", 4, 1),
    ("G", 7, 4), ("G", 1, 9), ("P", 0), ("G", 5, 1), ("G", 6, 7), ("G", 6, 6), ("G", 7, 7),
    ("G", 7, 6), ("A", 0, 0), ("G", 2, 9), ("G", 3, 9), ("A", 0, 1), ("G", 4, 2), ("G", 6, 8),
    ("G", 7, 8), ("M", 0, 0), ("G", 4, 5), ("G", 5, 5), ("T", 0, 0), ("T", 1, 0), ("M", 0, 1),
    ("G", 4, 3), ("G", 5, 3), ("P", 1), ("G", 4, 4), ("G", 5, 2), ("T", 0, 1), ("T", 1, 1),
    ("G", 6, 9), ("G", 7, 9), ("A", 1, 0), ("G", 4, 6), ("T", 1, 2), ("A", 1, 1), ("T", 0, 3),
    ("T", 1, 3), ("T", 0, 2), ("M", 1, 0), ("G", 5, 7), ("G", 5, 4), ("T", 2, 0), ("T", 3, 0),
    ("M", 1, 1), ("G", 4, 8), ("P", 3), ("T", 0, 7), ("T", 1, 7), ("G", 4, 7), ("T", 0, 6),
    ("T", 1, 6), ("G", 5, 6), ("T", 2, 1), ("T", 3, 1), ("A", 3, 0), ("A", 3, 1), ("G", 5, 8),
    ("T", 2, 3), ("T", 2, 2), ("T", 3, 3), ("T", 3, 2), ("T", 0, 5), ("M", 3, 0), ("T", 1, 5),
    ("T", 6, 0), ("T", 7, 0), ("M", 3, 1), ("G", 4, 9), ("T", 0, 4), ("T", 2, 7), ("T", 2, 6),
    ("T", 3, 7), ("T", 3, 6), ("T", 1, 4), ("T", 6, 1), ("G", 5, 9), ("P", 2), ("T", 2, 5),
    ("T", 3, 5), ("T", 7, 1), ("A", 2, 0), ("T", 2, 4), ("T", 6, 3), ("T", 7, 3), ("T", 6, 2),
    ("T", 7, 2), ("A", 2, 1), ("T", 0, 8), ("T", 0, 9), ("T", 1, 8), ("T", 1, 9), ("T", 3, 4),
    ("T", 6, 7), ("T", 6, 6), ("T", 7, 7), ("T", 7, 6), ("M", 2, 0), ("T", 4, 0), ("T", 5, 0),
    ("M", 2, 1), ("T", 4, 1), ("T", 2, 8), ("T", 2, 9), ("T", 0, 10), ("T", 6, 5), ("T", 7, 5),
    ("T", 5, 1), ("T", 6, 4), ("T", 7, 4), ("T", 1, 10), ("T", 3, 8), ("T", 3, 9), ("T", 4, 2),
    ("T", 5, 2), ("T", 4, 3), ("T", 5, 3), ("T", 2, 10), ("T", 4, 7), ("T", 4, 6), ("T", 0, 11),
    ("T", 6, 8), ("T", 6, 9), ("T", 5, 6), ("T", 5, 7), ("T", 7, 8), ("T", 1, 11), ("T", 3, 10),
    ("T", 7, 9), ("T", 0, 12), ("T", 4, 4), ("T", 5, 4), ("T", 4, 5), ("T", 5, 5), ("T", 2, 11),
    ("T", 1, 12), ("T", 6, 10), ("T", 7, 10), ("T", 3, 11), ("T", 4, 8), ("T", 6, 11),
    ("T", 2, 12), ("T", 5, 8), ("T", 7, 11), ("T", 4, 9), ("T", 3, 12), ("T", 4, 10), ("T", 6, 12),
    ("T", 5, 9), ("T", 5, 10), ("T", 7, 12), ("T", 4, 11), ("T", 5, 11), ("T", 4, 12),
    ("T", 5, 12),
)


def step(*arrays):
    hbm, vm = pl.BlockSpec(memory_space=pl.ANY), pl.BlockSpec(memory_space=pltpu.VMEM)
    return pl.pallas_call(
        step_kernel,
        out_shape=(
            jax.ShapeDtypeStruct((ROWS, KVC), F32),
            jax.ShapeDtypeStruct((ROWS, KVC), F32),
        ),
        in_specs=[hbm] * 6,
        out_specs=(vm, vm),
        scratch_shapes=[
            pltpu.VMEM((1, D), F32),
            pltpu.VMEM((ROWS, KVC), BF),
            pltpu.VMEM((ROWS, KVC), F32),
            pltpu.VMEM((TOK, 2560), BF),
            pltpu.VMEM((TOK, 2560), BF),
            pltpu.VMEM((TOK, D), BF),
            pltpu.VMEM((D, TOK), BF),
            pltpu.VMEM((8, 2, 4, 4, ROWS, 128), BF),
            pltpu.VMEM((TOK, 256), F32),
            pltpu.VMEM((TOK, KVC), BF),
            pltpu.VMEM((4, TOK, 256), BF),
            pltpu.VMEM((256, 1280), BF),
            pltpu.VMEM((256, 1280), BF),
            pltpu.VMEM((8, 2, 4, 4, ROWS, 128), BF),
            pltpu.VMEM((8, 4, 2, ROWS, 128), BF),
            pltpu.VMEM((8, 8, 2, ROWS, 128), BF),
            pltpu.VMEM((8, 2, 2, ROWS, 128), BF),
            pltpu.VMEM((8, 3, ROWS, 128), BF),
            pltpu.VMEM((4, 8, ROWS, 128), BF),
            pltpu.VMEM((4, ROWS, 128), BF),
            pltpu.VMEM((ROWS, 128), F32),
            pltpu.SemaphoreType.DMA((8, 17)),
            pltpu.SemaphoreType.DMA((8, 17)),
            pltpu.SemaphoreType.DMA((8, 17)),
            pltpu.SemaphoreType.DMA((8, 17)),
            pltpu.SemaphoreType.DMA((9, 3)),
            pltpu.SemaphoreType.DMA((9, 3)),
            pltpu.SemaphoreType.DMA((8,)),
            pltpu.SemaphoreType.DMA((8,)),
            pltpu.SemaphoreType.DMA((5,)),
        ],
        compiler_params=pltpu.CompilerParams(
            collective_id=0, has_side_effects=True, vmem_limit_bytes=67043328
        ),
    )(*arrays)


def local(hidden, norm_gain, queries, out_grad, kv_inner, kv_outer, momentum):
    fresh, average = step(
        hidden[0].reshape(TOK, D),
        norm_gain.reshape(1, D),
        kv_inner[0],
        queries[0].reshape(TOK, -1),
        out_grad[0].reshape(TOK, -1),
        kv_outer,
    )
    moment_new = momentum_decay * momentum + average
    outer_new = kv_outer - outer_rate * (momentum_decay * moment_new + average)
    blended = (blend_share * fresh + (1.0 - blend_share) * outer_new).astype(BF)
    return (blended[None], outer_new, moment_new)


def solution(mesh):
    split = Mesh(
        mesh.devices.reshape(2, 2, 2, 4, 4), GROUP + FSDP
    )
    return jax.shard_map(
        local,
        mesh=split,
        in_specs=(
            P(GROUP, FSDP, None, None),
            P(),
            P(GROUP, FSDP, None, None),
            P(GROUP, FSDP, None, None),
            P(GROUP, FSDP, None),
            P(FSDP, None),
            P(FSDP, None),
        ),
        out_specs=(P(GROUP, FSDP, None), P(FSDP, None), P(FSDP, None)),
        check_vma=False,
    )
```

time: 167 us -> 133 us (0.80)
  Pallas kernels: 157 us -> 129 us
  local copies, waits for them, and re-layouts: 8.39 us -> 0 us
  other arithmetic: 0 us -> 3.16 us
    pallas_call x2 -> x1, Pallas kernels: 157 us -> 129 us  [step(): pl.pallas_call(step_kernel, out_shape=(jax.ShapeDtypeStruct((ROWS, KVC),...]
    unnamed x9 -> x0, local copies, waits for them, and re-layouts: 8.39 us -> none
    broadcast_in_dim x0 -> x1, other arithmetic: none -> 3.16 us  [local(): return (blended[None], outer_new, moment_new)]
where the time goes in v3:
time: 133 us
  Pallas kernels  129 us (97%)
  other arithmetic  3.16 us (2%)
    pallas_call x1, Pallas kernels, step(): pl.pallas_call(step_kernel, out_shape=(jax.ShapeDtypeStruct((ROWS, KVC),...  129 us
    broadcast_in_dim x1, other arithmetic, local(): return (blended[None], outer_new, moment_new)  3.16 us

profile of v3, /device:TPU:1, one launch (start us, length us, event | category | flops | bytes accessed | tf_op | source)
XLA Modules:
  0.0 132.9 jit_solution(15206348671812096374)
XLA Ops:
  0.6 129.1 %shard_map.94 = (f32[160,1024]{1,0:T(8,128)}, f32[160,1024]{1,0:T(8,128)}) custom-call(bf16[512,5120]{1,0:T(8,128)(2,1)} %bitcast.7, f32[1,5120]{1,0:T(1,128)} %bitcast.11, bf16[160,1024]{1,0:T(8,128)(2,1)} %bitcast.10, bf16[512,2560]{1,0:T(8,128)(2,1)} %bitcast.8, bf16[512,2560]{1,0:T(8,128)(2,1)} %bitcast.9, f32[160,1024]{1,0:T(8,128)} %outer_any.1), custom_call_target="tpu_custom_call" | custom-call | tf_op jit(solution)/shard_map/pallas_call | solution.py:539
  129.7 3.2 %fusion = (bf16[1,160,1024]{2,1,0:T(8,128)(2,1)}, f32[160,1024]{1,0:T(8,128)}, f32[160,1024]{1,0:T(8,128)}) fusion(f32[160,1024]{1,0:T(8,128)} %get-tuple-element.5, f32[160,1024]{1,0:T(8,128)} %outer_any.1, f32[160,1024]{1,0:T(8,128)} %get-tuple-element.6, f32[160,1024]{1,0:T(8,128)} %param.13), kind=kLoop, calls=%fused_computation.3 | loop fusion | flops 1474560 | bytes 4259840 | tf_op jit(solution)/shard_map/broadcast_in_dim | solution.py:597

commit v4 on v3

--- a/solution.py
+++ b/solution.py
@@ -301,10 +301,16 @@
         if arriving:
             s = (self.slot(True, False), self.slot(False, True), self.slot(True, True))[k]
         else:
-            s = self.slot(k == 2, False)
+            s = self.slot(k == 2 and p not in DIRECT, False)
         ref = buf.at[s] if p == 8 else buf.at[s, p]
         dev = {"hi": 1 - self.hi} if k == 0 else {"core": 1 - self.core}
+        if k == 2 and p in DIRECT:
+            dev["hi"] = 1 - self.hi
         return remote(ref, ref, self.send.at[p, k], self.recv.at[p, k], dev)
+
+    def share(self, p):
+        for k in (0, 2, 1) if p in DIRECT else (0, 1):
+            self.copy(p, k, False).start()
 
     def code(self, p, grad):
         c = piece_cols(p)
@@ -317,19 +323,19 @@
         self.coded[self.slot(False, False), p] = (delta / scale).astype(BF)
         lane = lax.broadcasted_iota(jnp.int32, self.mine.shape, 1)
         self.mine[...] = jnp.where(lane == p, scale, self.mine[...])
-        self.copy(p, 0, False).start()
-        self.copy(p, 1, False).start()
+        self.share(p)
 
     def send_scales(self):
         self.scales[self.slot(False, False)] = self.mine[...].astype(BF)
-        self.copy(8, 0, False).start()
-        self.copy(8, 1, False).start()
+        self.share(8)
 
     def forward(self, p):
         self.copy(p, 0, True).wait_recv()
         self.copy(p, 2, False).start()
 
     def arrived(self, p):
+        if p in DIRECT:
+            self.copy(p, 0, True).wait_recv()
         self.copy(p, 1, True).wait_recv()
         self.copy(p, 2, True).wait_recv()
 
@@ -444,6 +450,7 @@
         cp.start()
     meet(
         [{"lo": pc.yo}, {"hi": 1 - ex.hi}, {"core": 1 - ex.core}]
+        + [{"hi": 1 - ex.hi, "core": 1 - ex.core}]
         + [pc.dev(p, True, o) for p in range(2) for o in (1, -1)]
     )
     for p in range(8):
@@ -485,7 +492,6 @@
     for kind, *nums in ORDER:
         acts[kind](*nums)
     ex.send_scales()
-    ex.forward(8)
     for p in range(8):
         ex.arrived(p)
     ex.arrived(8)
@@ -496,41 +502,42 @@
     ex.drain()
 
 
-LATE_Y = (4, 5)
+LATE_Y = (4, 5,)
+
+DIRECT = (6, 7, 8)
 
 ORDER = (
-    ("G", 0, 0), ("G", 1, 0), ("G", 2, 0), ("G", 3, 0), ("G", 4, 0), ("G", 5, 0), ("G", 6, 0),
-    ("G", 7, 0), ("N", 0), ("N", 1), ("N", 2), ("G", 0, 1), ("G", 1, 1), ("G", 2, 1), ("G", 3, 1),
-    ("N", 3), ("N", 4), ("G", 0, 2), ("N", 5), ("G", 0, 5), ("G", 0, 3), ("N", 6), ("G", 1, 5),
-    ("G", 1, 2), ("N", 7), ("G", 1, 3), ("G", 2, 5), ("G", 3, 5), ("U", 0), ("G", 2, 2), ("U", 1),
-    ("U", 2), ("G", 0, 6), ("G", 3, 2), ("U", 3), ("G", 1, 6), ("G", 2, 3), ("U", 4), ("G", 3, 3),
-    ("U", 5), ("U", 6), ("G", 0, 4), ("G", 7, 1), ("U", 7), ("C",), ("G", 2, 6), ("G", 3, 6),
-    ("G", 0, 7), ("G", 1, 7), ("G", 6, 1), ("G", 1, 4), ("G", 2, 4), ("G", 3, 4), ("G", 0, 8),
-    ("G", 2, 7), ("G", 3, 7), ("G", 6, 3), ("G", 7, 5), ("G", 6, 2), ("G", 7, 3), ("G", 1, 8),
-    ("G", 6, 5), ("G", 2, 8), ("G", 7, 2), ("G", 3, 8), ("G", 6, 4), ("G", 0, 9), ("G", 4, 1),
-    ("G", 7, 4), ("G", 1, 9), ("P", 0), ("G", 5, 1), ("G", 6, 7), ("G", 6, 6), ("G", 7, 7),
-    ("G", 7, 6), ("A", 0, 0), ("G", 2, 9), ("G", 3, 9), ("A", 0, 1), ("G", 4, 2), ("G", 6, 8),
-    ("G", 7, 8), ("M", 0, 0), ("G", 4, 5), ("G", 5, 5), ("T", 0, 0), ("T", 1, 0), ("M", 0, 1),
-    ("G", 4, 3), ("G", 5, 3), ("P", 1), ("G", 4, 4), ("G", 5, 2), ("T", 0, 1), ("T", 1, 1),
-    ("G", 6, 9), ("G", 7, 9), ("A", 1, 0), ("G", 4, 6), ("T", 1, 2), ("A", 1, 1), ("T", 0, 3),
-    ("T", 1, 3), ("T", 0, 2), ("M", 1, 0), ("G", 5, 7), ("G", 5, 4), ("T", 2, 0), ("T", 3, 0),
-    ("M", 1, 1), ("G", 4, 8), ("P", 3), ("T", 0, 7), ("T", 1, 7), ("G", 4, 7), ("T", 0, 6),
-    ("T", 1, 6), ("G", 5, 6), ("T", 2, 1), ("T", 3, 1), ("A", 3, 0), ("A", 3, 1), ("G", 5, 8),
-    ("T", 2, 3), ("T", 2, 2), ("T", 3, 3), ("T", 3, 2), ("T", 0, 5), ("M", 3, 0), ("T", 1, 5),
-    ("T", 6, 0), ("T", 7, 0), ("M", 3, 1), ("G", 4, 9), ("T", 0, 4), ("T", 2, 7), ("T", 2, 6),
-    ("T", 3, 7), ("T", 3, 6), ("T", 1, 4), ("T", 6, 1), ("G", 5, 9), ("P", 2), ("T", 2, 5),
-    ("T", 3, 5), ("T", 7, 1), ("A", 2, 0), ("T", 2, 4), ("T", 6, 3), ("T", 7, 3), ("T", 6, 2),
-    ("T", 7, 2), ("A", 2, 1), ("T", 0, 8), ("T", 0, 9), ("T", 1, 8), ("T", 1, 9), ("T", 3, 4),
-    ("T", 6, 7), ("T", 6, 6), ("T", 7, 7), ("T", 7, 6), ("M", 2, 0), ("T", 4, 0), ("T", 5, 0),
-    ("M", 2, 1), ("T", 4, 1), ("T", 2, 8), ("T", 2, 9), ("T", 0, 10), ("T", 6, 5), ("T", 7, 5),
-    ("T", 5, 1), ("T", 6, 4), ("T", 7, 4), ("T", 1, 10), ("T", 3, 8), ("T", 3, 9), ("T", 4, 2),
-    ("T", 5, 2), ("T", 4, 3), ("T", 5, 3), ("T", 2, 10), ("T", 4, 7), ("T", 4, 6), ("T", 0, 11),
-    ("T", 6, 8), ("T", 6, 9), ("T", 5, 6), ("T", 5, 7), ("T", 7, 8), ("T", 1, 11), ("T", 3, 10),
-    ("T", 7, 9), ("T", 0, 12), ("T", 4, 4), ("T", 5, 4), ("T", 4, 5), ("T", 5, 5), ("T", 2, 11),
-    ("T", 1, 12), ("T", 6, 10), ("T", 7, 10), ("T", 3, 11), ("T", 4, 8), ("T", 6, 11),
-    ("T", 2, 12), ("T", 5, 8), ("T", 7, 11), ("T", 4, 9), ("T", 3, 12), ("T", 4, 10), ("T", 6, 12),
-    ("T", 5, 9), ("T", 5, 10), ("T", 7, 12), ("T", 4, 11), ("T", 5, 11), ("T", 4, 12),
-    ("T", 5, 12),
+    ("G", 1, 0), ("G", 0, 0), ("G", 3, 0), ("G", 2, 0), ("G", 4, 0), ("G", 5, 0), ("C",),
+    ("G", 6, 0), ("N", 0), ("N", 1), ("G", 1, 1), ("G", 0, 1), ("N", 2), ("G", 3, 1), ("G", 2, 1),
+    ("N", 3), ("G", 1, 2), ("G", 7, 0), ("N", 4), ("G", 1, 3), ("N", 5), ("G", 1, 5), ("G", 0, 2),
+    ("G", 0, 5), ("N", 6), ("G", 0, 3), ("G", 2, 5), ("G", 3, 2), ("N", 7), ("G", 3, 3),
+    ("G", 2, 2), ("U", 0), ("U", 7), ("G", 1, 6), ("U", 4), ("G", 0, 6), ("G", 2, 3), ("G", 3, 5),
+    ("U", 3), ("U", 1), ("U", 5), ("G", 1, 7), ("G", 6, 1), ("U", 2), ("U", 6), ("G", 1, 4),
+    ("G", 3, 6), ("G", 2, 6), ("G", 0, 7), ("G", 3, 4), ("G", 0, 4), ("G", 3, 7), ("G", 2, 4),
+    ("G", 7, 1), ("G", 2, 7), ("G", 1, 8), ("G", 5, 1), ("G", 6, 5), ("G", 7, 3), ("G", 0, 8),
+    ("G", 3, 8), ("G", 6, 3), ("G", 2, 8), ("G", 7, 2), ("G", 6, 2), ("G", 1, 9), ("G", 0, 9),
+    ("G", 4, 1), ("G", 7, 5), ("P", 0), ("G", 5, 2), ("G", 5, 5), ("A", 0, 0), ("G", 2, 9),
+    ("G", 5, 3), ("G", 6, 4), ("A", 0, 1), ("G", 3, 9), ("G", 7, 4), ("G", 6, 7), ("G", 6, 6),
+    ("M", 0, 0), ("G", 4, 5), ("G", 4, 2), ("G", 7, 6), ("G", 7, 7), ("T", 0, 0), ("M", 0, 1),
+    ("G", 5, 4), ("G", 6, 8), ("T", 1, 0), ("P", 1), ("G", 4, 3), ("G", 5, 6), ("G", 7, 8),
+    ("A", 1, 0), ("G", 4, 4), ("T", 1, 1), ("T", 0, 1), ("A", 1, 1), ("G", 5, 8), ("M", 1, 0),
+    ("G", 4, 6), ("T", 0, 2), ("T", 1, 2), ("T", 0, 3), ("M", 1, 1), ("G", 5, 7), ("T", 1, 3),
+    ("G", 6, 9), ("T", 3, 0), ("T", 2, 0), ("G", 7, 9), ("P", 3), ("G", 4, 8), ("T", 1, 7),
+    ("T", 0, 7), ("T", 1, 6), ("A", 3, 0), ("G", 4, 7), ("T", 0, 6), ("T", 3, 1), ("A", 3, 1),
+    ("T", 1, 5), ("T", 2, 1), ("M", 3, 0), ("T", 0, 4), ("M", 3, 1), ("G", 5, 9), ("T", 0, 5),
+    ("T", 3, 2), ("T", 3, 3), ("T", 2, 3), ("T", 2, 2), ("T", 7, 0), ("T", 6, 0), ("T", 1, 4),
+    ("G", 4, 9), ("P", 2), ("T", 2, 7), ("T", 2, 6), ("T", 3, 7), ("T", 3, 6), ("A", 2, 0),
+    ("T", 0, 8), ("T", 6, 1), ("A", 2, 1), ("T", 0, 9), ("T", 2, 4), ("T", 2, 5), ("T", 3, 4),
+    ("M", 2, 0), ("T", 1, 8), ("T", 3, 5), ("T", 1, 9), ("T", 7, 2), ("T", 7, 3), ("T", 5, 0),
+    ("T", 6, 3), ("M", 2, 1), ("T", 6, 2), ("T", 5, 1), ("T", 4, 0), ("T", 7, 5), ("T", 7, 4),
+    ("T", 0, 10), ("T", 2, 8), ("T", 6, 7), ("T", 3, 8), ("T", 2, 9), ("T", 5, 2), ("T", 6, 6),
+    ("T", 5, 3), ("T", 1, 10), ("T", 3, 9), ("T", 6, 5), ("T", 7, 1), ("T", 6, 4), ("T", 4, 1),
+    ("T", 5, 6), ("T", 4, 2), ("T", 5, 7), ("T", 4, 3), ("T", 0, 11), ("T", 2, 10), ("T", 3, 10),
+    ("T", 5, 4), ("T", 1, 11), ("T", 6, 8), ("T", 6, 9), ("T", 5, 5), ("T", 7, 6), ("T", 4, 6),
+    ("T", 7, 7), ("T", 4, 7), ("T", 0, 12), ("T", 5, 8), ("T", 4, 4), ("T", 2, 11), ("T", 5, 9),
+    ("T", 4, 5), ("T", 3, 11), ("T", 6, 10), ("T", 1, 12), ("T", 7, 8), ("T", 7, 9), ("T", 5, 10),
+    ("T", 4, 8), ("T", 6, 11), ("T", 7, 10), ("T", 4, 9), ("T", 4, 10), ("T", 5, 11), ("T", 2, 12),
+    ("T", 7, 11), ("T", 4, 11), ("T", 3, 12), ("T", 5, 12), ("T", 4, 12),
 )
 
 

time: 133 us -> 127 us (0.955)
  Pallas kernels: 129 us -> 123 us
    pallas_call x1, Pallas kernels: 129 us -> 123 us  [step(): pl.pallas_call(step_kernel, out_shape=(jax.ShapeDtypeStruct((ROWS, KVC),...]
where the time goes in v4:
time: 127 us
  Pallas kernels  123 us (97%)
  other arithmetic  3.16 us (2%)
    pallas_call x1, Pallas kernels, step(): pl.pallas_call(step_kernel, out_shape=(jax.ShapeDtypeStruct((ROWS, KVC),...  123 us
    broadcast_in_dim x1, other arithmetic, local(): return (blended[None], outer_new, moment_new)  3.16 us

profile of v4, /device:TPU:1, one launch (start us, length us, event | category | flops | bytes accessed | tf_op | source)
XLA Modules:
  0.0 126.6 jit_solution(12782858211674018002)
XLA Ops:
  0.6 122.8 %shard_map.94 = (f32[160,1024]{1,0:T(8,128)}, f32[160,1024]{1,0:T(8,128)}) custom-call(bf16[512,5120]{1,0:T(8,128)(2,1)} %bitcast.7, f32[1,5120]{1,0:T(1,128)} %bitcast.11, bf16[160,1024]{1,0:T(8,128)(2,1)} %bitcast.10, bf16[512,2560]{1,0:T(8,128)(2,1)} %bitcast.8, bf16[512,2560]{1,0:T(8,128)(2,1)} %bitcast.9, f32[160,1024]{1,0:T(8,128)} %outer_any.1), custom_call_target="tpu_custom_call" | custom-call | tf_op jit(solution)/shard_map/pallas_call | solution.py:546
  123.4 3.2 %fusion = (bf16[1,160,1024]{2,1,0:T(8,128)(2,1)}, f32[160,1024]{1,0:T(8,128)}, f32[160,1024]{1,0:T(8,128)}) fusion(f32[160,1024]{1,0:T(8,128)} %get-tuple-element.5, f32[160,1024]{1,0:T(8,128)} %outer_any.1, f32[160,1024]{1,0:T(8,128)} %get-tuple-element.6, f32[160,1024]{1,0:T(8,128)} %param.13), kind=kLoop, calls=%fused_computation.3 | loop fusion | flops 1474560 | bytes 4259840 | tf_op jit(solution)/shard_map/broadcast_in_dim | solution.py:604

commit v5 on v4

--- a/solution.py
+++ b/solution.py
@@ -584,7 +584,7 @@
             pltpu.SemaphoreType.DMA((5,)),
         ],
         compiler_params=pltpu.CompilerParams(
-            collective_id=0, has_side_effects=True, vmem_limit_bytes=67043328
+            collective_id=0, has_side_effects=True, vmem_limit_bytes=60000000
         ),
     )(*arrays)
 

time: 127 us -> 126 us (level)
  no operation moved by 1% of the time
where the time goes in v5:
time: 126 us
  Pallas kernels  123 us (98%)
  other arithmetic  2.68 us (2%)
    pallas_call x1, Pallas kernels, step(): pl.pallas_call(step_kernel, out_shape=(jax.ShapeDtypeStruct((ROWS, KVC),...  123 us
    broadcast_in_dim x1, other arithmetic, local(): return (blended[None], outer_new, moment_new)  2.68 us

profile of v5, /device:TPU:1, one launch (start us, length us, event | category | flops | bytes accessed | tf_op | source)
XLA Modules:
  0.0 126.1 jit_solution(2100713239978021601)
XLA Ops:
  0.6 0.0 copy-start
  0.6 0.0 copy-start.1
  0.7 122.7 %shard_map.94 = (f32[160,1024]{1,0:T(8,128)}, f32[160,1024]{1,0:T(8,128)}) custom-call(bf16[512,5120]{1,0:T(8,128)(2,1)} %bitcast.7, f32[1,5120]{1,0:T(1,128)} %bitcast.11, bf16[160,1024]{1,0:T(8,128)(2,1)} %bitcast.10, bf16[512,2560]{1,0:T(8,128)(2,1)} %bitcast.8, bf16[512,2560]{1,0:T(8,128)(2,1)} %bitcast.9, f32[160,1024]{1,0:T(8,128)} %outer_any.1), custom_call_target="tpu_custom_call" | custom-call | tf_op jit(solution)/shard_map/pallas_call | solution.py:546
  123.4 0.0 copy-done
  123.4 0.0 copy-done.1
  123.4 2.7 %fusion = (bf16[1,160,1024]{2,1,0:T(8,128)(2,1)}, f32[160,1024]{1,0:T(8,128)}, f32[160,1024]{1,0:T(8,128)}) fusion(f32[160,1024]{1,0:T(8,128)} %get-tuple-element.5, f32[160,1024]{1,0:T(8,128)S(1)} %copy-done, f32[160,1024]{1,0:T(8,128)} %get-tuple-element.6, f32[160,1024]{1,0:T(8,128)S(1)} %copy-done.1), kind=kLoop, calls=%fused_computation.3 | loop fusion | flops 1474560 | bytes 4259840 | tf_op jit(solution)/shard_map/broadcast_in_dim | solution.py:604
Async XLA Ops:
  0.6 122.8 %copy-start = (f32[160,1024]{1,0:T(8,128)S(1)}, f32[160,1024]{1,0:T(8,128)}, u32[]{:S(2)}) copy-start(f32[160,1024]{1,0:T(8,128)} %outer_any.1) | copy-start | bytes 1966084
  0.6 122.8 %copy-start.1 = (f32[160,1024]{1,0:T(8,128)S(1)}, f32[160,1024]{1,0:T(8,128)}, u32[]{:S(2)}) copy-start(f32[160,1024]{1,0:T(8,128)} %param.13) | copy-start | bytes 1966084
